TPU v7x, 256 devices: a whole 4x4x8 slice. The times are simulated.
256 devices in a mesh: band: 8 (over y, z_hi), domain: 32 (over z_lo, x, core).
Axes of the slice: x: 4, y: 4, z: 8 (z_hi: 2, z_lo: 4; z = z_hi * 4 + z_lo), core: 2. Of those that a mesh axis runs over, the one named last changes fastest.
Arguments:
- orbital_block: bfloat16 [256, 384, 16, 128], P('band', 'domain'), may hold values from -8 to 8
- block_scale: float32 [256, 384], P('band', 'domain'), may hold values from 0.5 to 6
- potential: float32 [384, 16, 128], P('domain'), may hold values from -4 to 0
Outputs:
- orthonormal: bfloat16 [256, 384, 16, 128], P('band', 'domain')
All inputs are finite; a program needn't handle non-finite values.
Results may differ from a plain program's by a relative error of at most 0.015.
Values may be sent and summed in bfloat16 or wider, within the bound.
A program may use at most 64 MiB of HBM per device.

v0:
```python
import jax
import jax.numpy as jnp
from jax import lax
from jax.sharding import PartitionSpec as P

grid_step = 0.5
stencil_coef = (
    -5369.0 / 1800.0,
    12.0 / 7.0,
    -15.0 / 56.0,
    10.0 / 189.0,
    -1.0 / 112.0,
    2.0 / 1925.0,
    -1.0 / 16632.0,
)
lower_end = -4.0
cut_energy = 6.0
upper_end = 43.0


def padded_2(block, sides, width):
    for axis, dim in sides:
        count = lax.axis_size(axis)
        forward = [(i, i + 1) for i in range(count - 1)]
        backward = [(target, source) for source, target in forward]
        low = lax.ppermute(
            lax.slice_in_dim(block, block.shape[dim] - width, None, axis=dim), axis, forward
        )
        high = lax.ppermute(lax.slice_in_dim(block, 0, width, axis=dim), axis, backward)
        block = jnp.concatenate([low, block, high], axis=dim)
    return block


def filter_terms():
    width_e = (upper_end - cut_energy) / 2.0
    centre = (upper_end + cut_energy) / 2.0
    sigma_one = width_e / (lower_end - centre)
    gamma_term = 2.0 / sigma_one
    sigma_two = 1.0 / (gamma_term - sigma_one)
    sigma_three = 1.0 / (gamma_term - sigma_two)
    return (width_e, centre, sigma_one, sigma_two, sigma_three)


def hamiltonian(padded, potential):
    count_x = padded.shape[1] - 12
    count_y = padded.shape[2] - 12
    count_z = padded.shape[3] - 12

    def window(shift_x, shift_y, shift_z):
        return padded[
            :,
            6 + shift_x : 6 + shift_x + count_x,
            6 + shift_y : 6 + shift_y + count_y,
            6 + shift_z : 6 + shift_z + count_z,
        ].astype(jnp.float32)

    kinetic = -0.5 / (grid_step * grid_step)
    result = (3.0 * stencil_coef[0] * kinetic + potential[None]) * window(0, 0, 0)
    for offset in range(1, 7):
        neighbours = (
            window(offset, 0, 0)
            + window(-offset, 0, 0)
            + window(0, offset, 0)
            + window(0, -offset, 0)
            + window(0, 0, offset)
            + window(0, 0, -offset)
        )
        result = result + kinetic * stencil_coef[offset] * neighbours
    return result


def body(orbital_block, block_scale, potential):
    band_rows, planes, rows_y, rows_z = orbital_block.shape
    width_e, centre, sigma_one, sigma_two, sigma_three = filter_terms()
    scaled = (orbital_block.astype(jnp.float32) * block_scale[:, :, None, None]).astype(
        jnp.bfloat16
    )

    def centred(extended, energies):
        padded = jnp.pad(extended, ((0, 0), (0, 0), (6, 6), (6, 6)))
        middle = extended[:, 6 : extended.shape[1] - 6].astype(jnp.float32)
        return hamiltonian(padded, energies) - centre * middle

    def extend(source_field):
        return padded_2(source_field, (("domain", 1),), 6)

    first_iter = (centred(extend(scaled), potential) * (sigma_one / width_e)).astype(jnp.bfloat16)
    second = (
        2.0 * sigma_two / width_e * centred(extend(first_iter), potential)
        - sigma_one * sigma_two * scaled.astype(jnp.float32)
    ).astype(jnp.bfloat16)
    third_iter = (
        2.0 * sigma_three / width_e * centred(extend(second), potential)
        - sigma_two * sigma_three * first_iter.astype(jnp.float32)
    ).astype(jnp.bfloat16)
    cell_count = planes * rows_y * rows_z
    flattened = third_iter.reshape(band_rows, cell_count)
    columns = lax.all_to_all(flattened, "band", split_axis=1, concat_axis=0, tiled=True)
    partial_gram = lax.dot_general(
        columns, columns, (((1,), (1,)), ((), ())), preferred_element_type=jnp.float32
    )
    gram_sum = lax.psum(partial_gram, ("band", "domain"))
    correlation = gram_sum / float(cell_count * lax.axis_size("domain"))
    lower_factor = jnp.linalg.cholesky(correlation)
    inverse = jax.scipy.linalg.solve_triangular(
        lower_factor, jnp.eye(correlation.shape[0], dtype=jnp.float32), lower=True
    )
    rotation = inverse.astype(jnp.bfloat16)
    mixed = jnp.dot(rotation, columns, preferred_element_type=jnp.float32).astype(jnp.bfloat16)
    returned = lax.all_to_all(mixed, "band", split_axis=0, concat_axis=1, tiled=True)
    return returned.reshape(band_rows, planes, rows_y, rows_z)


def solution(mesh):
    in_specs = (P("band", "domain", None, None), P("band", "domain"), P("domain", None, None))
    out_specs = P("band", "domain", None, None)
    return jax.shard_map(body, mesh=mesh, in_specs=in_specs, out_specs=out_specs, check_vma=False)
```

profile of v0, /device:TPU:64, one launch (start us, length us, event | category | flops | bytes accessed | tf_op | source)
XLA Modules:
  0.0 559.7 jit_solution(8117295497307411738)
XLA Ops:
  7.3 1.9 multiply_convert_fusion
  9.5 3.7 collective-permute-start
  13.2 1.9 collective-permute-start.1
  15.1 7.5 %collective-permute-done = bf16[32,6,16,128]{3,2,1,0:T(8,128)(2,1)S(1)} collective-permute-done((bf16[32,6,16,128]{3,2,1,0:T(8,128)(2,1)S(1)}, bf16[32,6,16,128]{3,2,1,0:T(8,128)(2,1)S(1)}, u32[]{:S(2)}, u32[]{:S(2)}) %collective-permute-start) | collective-permute-done | bytes 786464 | tf_op jit(solution)/shard_map/ppermute | solution.py:29
  22.7 5.9 %collective-permute-done.1 = bf16[32,6,16,128]{3,2,1,0:T(8,128)(2,1)S(1)} collective-permute-done((bf16[32,6,16,128]{3,2,1,0:T(8,128)(2,1)S(1)}, bf16[32,6,16,128]{3,2,1,0:T(8,128)(2,1)S(1)}, u32[]{:S(2)}, u32[]{:S(2)}) %collective-permute-start.1) | collective-permute-done | bytes 786464 | tf_op jit(solution)/shard_map/ppermute | solution.py:26
  28.6 8.7 %select_maximum_fusion.4 = bf16[32,24,28,140]{3,2,1,0:T(8,128)(2,1)S(1)} fusion(bf16[32,6,16,128]{3,2,1,0:T(8,128)(2,1)S(1)} %collective-permute-done, bf16[32,12,16,128]{3,2,1,0:T(8,128)(2,1)S(1)} %multiply_convert_fusion, bf16[32,6,16,128]{3,2,1,0:T(8,128)(2,1)S(1)} %collective-permute-done.1), kind=kLoop, calls=%fused_computation.13 | loop fusion | flops 57200640 | bytes 9166848 | tf_op jit(solution)/shard_map/concatenate | solution.py:30
  37.3 19.2 %fusion.21 = bf16[32,12,16,128]{3,2,1,0:T(8,128)(2,1)S(1)} fusion(bf16[32,12,16,128]{3,2,1,0:T(8,128)(2,1)S(1)} %multiply_convert_fusion, bf16[32,6,16,128]{3,2,1,0:T(8,128)(2,1)S(1)} %collective-permute-done.1, bf16[32,6,16,128]{3,2,1,0:T(8,128)(2,1)S(1)} %collective-permute-done, bf16[32,24,28,140]{3,2,1,0:T(8,128)(2,1)S(1)} %select_maximum_fusion.4, ...), kind=kLoop, calls=%fused_computation.72 | loop fusion | flops 75497472 | bytes 42565632 | tf_op jit(solution)/shard_map/convert_element_type | solution.py:87
  56.8 1.9 collective-permute-start.2
  58.7 2.5 collective-permute-start.3
  61.3 6.9 %collective-permute-done.2 = bf16[32,6,16,128]{3,2,1,0:T(8,128)(2,1)S(1)} collective-permute-done((bf16[32,6,16,128]{3,2,1,0:T(8,128)(2,1)S(1)}, bf16[32,6,16,128]{3,2,1,0:T(8,128)(2,1)S(1)}, u32[]{:S(2)}, u32[]{:S(2)}) %collective-permute-start.2) | collective-permute-done | bytes 786464 | tf_op jit(solution)/shard_map/ppermute | solution.py:29
  68.2 6.1 %collective-permute-done.3 = bf16[32,6,16,128]{3,2,1,0:T(8,128)(2,1)S(1)} collective-permute-done((bf16[32,6,16,128]{3,2,1,0:T(8,128)(2,1)S(1)}, bf16[32,6,16,128]{3,2,1,0:T(8,128)(2,1)S(1)}, u32[]{:S(2)}, u32[]{:S(2)}) %collective-permute-start.3) | collective-permute-done | bytes 786464 | tf_op jit(solution)/shard_map/ppermute | solution.py:26
  74.3 8.7 %select_maximum_fusion.2 = bf16[32,24,28,140]{3,2,1,0:T(8,128)(2,1)S(1)} fusion(bf16[32,6,16,128]{3,2,1,0:T(8,128)(2,1)S(1)} %collective-permute-done.2, bf16[32,12,16,128]{3,2,1,0:T(8,128)(2,1)S(1)} %fusion.21, bf16[32,6,16,128]{3,2,1,0:T(8,128)(2,1)S(1)} %collective-permute-done.3), kind=kLoop, calls=%fused_computation.11 | loop fusion | flops 57200640 | bytes 9166848 | tf_op jit(solution)/shard_map/concatenate | solution.py:30
  83.0 19.7 %fusion.23 = bf16[32,12,16,128]{3,2,1,0:T(8,128)(2,1)S(1)} fusion(bf16[32,12,16,128]{3,2,1,0:T(8,128)(2,1)S(1)} %fusion.21, bf16[32,6,16,128]{3,2,1,0:T(8,128)(2,1)S(1)} %collective-permute-done.3, bf16[32,6,16,128]{3,2,1,0:T(8,128)(2,1)S(1)} %collective-permute-done.2, bf16[32,24,28,140]{3,2,1,0:T(8,128)(2,1)S(1)} %select_maximum_fusion.2, ...), kind=kLoop, calls=%fused_computation.74 | loop fusion | flops 80216064 | bytes 44140032 | tf_op jit(solution)/shard_map/convert_element_type | solution.py:91
  103.1 1.9 collective-permute-start.4
  105.0 2.4 collective-permute-start.5
  107.4 7.1 %collective-permute-done.4 = bf16[32,6,16,128]{3,2,1,0:T(8,128)(2,1)S(1)} collective-permute-done((bf16[32,6,16,128]{3,2,1,0:T(8,128)(2,1)S(1)}, bf16[32,6,16,128]{3,2,1,0:T(8,128)(2,1)S(1)}, u32[]{:S(2)}, u32[]{:S(2)}) %collective-permute-start.4) | collective-permute-done | bytes 786464 | tf_op jit(solution)/shard_map/ppermute | solution.py:29
  114.5 5.9 %collective-permute-done.5 = bf16[32,6,16,128]{3,2,1,0:T(8,128)(2,1)S(1)} collective-permute-done((bf16[32,6,16,128]{3,2,1,0:T(8,128)(2,1)S(1)}, bf16[32,6,16,128]{3,2,1,0:T(8,128)(2,1)S(1)}, u32[]{:S(2)}, u32[]{:S(2)}) %collective-permute-start.5) | collective-permute-done | bytes 786464 | tf_op jit(solution)/shard_map/ppermute | solution.py:26
  120.4 8.7 %select_maximum_fusion = bf16[32,24,28,140]{3,2,1,0:T(8,128)(2,1)S(1)} fusion(bf16[32,6,16,128]{3,2,1,0:T(8,128)(2,1)S(1)} %collective-permute-done.4, bf16[32,12,16,128]{3,2,1,0:T(8,128)(2,1)S(1)} %fusion.23, bf16[32,6,16,128]{3,2,1,0:T(8,128)(2,1)S(1)} %collective-permute-done.5), kind=kLoop, calls=%fused_computation.9 | loop fusion | flops 57200640 | bytes 9166848 | tf_op jit(solution)/shard_map/concatenate | solution.py:30
  129.2 19.6 %fusion.12 = bf16[32,12,16,128]{3,2,1,0:T(8,128)(2,1)S(1)} fusion(bf16[32,12,16,128]{3,2,1,0:T(8,128)(2,1)S(1)} %fusion.23, bf16[32,12,16,128]{3,2,1,0:T(8,128)(2,1)S(1)} %fusion.21, bf16[32,6,16,128]{3,2,1,0:T(8,128)(2,1)S(1)} %collective-permute-done.5, bf16[32,6,16,128]{3,2,1,0:T(8,128)(2,1)S(1)} %collective-permute-done.4, ...), kind=kLoop, calls=%fused_computation.63 | loop fusion | flops 77856768 | bytes 44138496 | tf_op jit(solution)/shard_map/convert_element_type | solution.py:95
  150.3 35.0 %all_to_all.35 = bf16[32,8,3072]{2,0,1:T(8,128)(2,1)S(1)} all-to-all(bf16[32,8,3072]{2,0,1:T(8,128)(2,1)S(1)} %copy.18), channel_id=1, replica_groups=mesh['band'=8,'domain'=32] {'band'}, dimensions={1} | all-to-all | bytes 3145728 | tf_op jit(solution)/shard_map/all_to_all | solution.py:98
  185.4 1.3 fusion.78
  186.8 258.0 %all-reduce.6.cloned.1.call-done = f32[256,256]{0,1:T(8,128)} async-done(((f32[256,256]{0,1:T(8,128)}), f32[256,256]{0,1:T(8,128)}) %all-reduce.6.cloned.1.call-update) | async-done | bytes 262160 | tf_op jit(solution)/shard_map/psum | solution.py:102
  445.9 1.0 fusion.62
  446.9 11.7 %cholesky.50 = f32[128,128]{1,0:T(8,128)S(1)} custom-call(f32[128,128]{1,0:T(8,128)S(1)} %cholesky.118), custom_call_target="Cholesky" | custom-call | tf_op jit(solution)/shard_map/jit(cholesky)/cholesky | solution.py:104
  458.7 9.8 %custom-call.15 = f32[1,128,128]{1,2,0:T(8,128)S(1)} custom-call(f32[1,128,128]{2,1,0:T(8,128)S(1)} %get-tuple-element.32), custom_call_target="InvertDiagBlocksLowerTriangular" | custom-call | tf_op jit(solution)/shard_map/jit(cholesky)/cholesky | solution.py:104
  469.0 11.7 %cholesky.105 = f32[128,128]{1,0:T(8,128)S(1)} custom-call(f32[128,128]{1,0:T(8,128)S(1)} %convolution_subtract_fusion.1), custom_call_target="Cholesky" | custom-call | tf_op jit(solution)/shard_map/jit(cholesky)/cholesky | solution.py:104
  482.9 4.1 while.1
  483.5 1.4 bitcast_dynamic-update-slice_fusion.2
  485.6 1.4 bitcast_dynamic-update-slice_fusion.2
  487.0 19.9 %custom-call.16 = f32[2,128,128]{1,2,0:T(8,128)S(1)} custom-call(f32[2,128,128]{2,1,0:T(8,128)S(1)} %get-tuple-element.12), custom_call_target="InvertDiagBlocksLowerTriangular" | custom-call | tf_op jit(solution)/shard_map/jit(_solve_triangular)/triangular_solve | solution.py:105
  508.4 42.0 %all_to_all.36 = bf16[8,32,3072]{2,1,0:T(8,128)(2,1)S(1)} all-to-all(bf16[8,32,3072]{2,1,0:T(8,128)(2,1)S(1)} %bitcast.45), channel_id=1, replica_groups=mesh['band'=8,'domain'=32] {'band'}, dimensions={0} | all-to-all | bytes 3145728 | tf_op jit(solution)/shard_map/all_to_all | solution.py:110
  551.2 1.6 reshape.34
  (36 shorter events, 9.2 us)
Async XLA Ops:
  6.5 438.3 %all-reduce.6.cloned.1.call-start = ((), (), s32[]{:S(2)}) async-start(), calls=%async_computation.2 | async-start | bytes 524288 | tf_op jit(solution)/shard_map/psum | solution.py:102
  7.3 7.8 %copy-start.1 = (f32[12,16,128]{2,1,0:T(8,128)S(1)}, f32[12,16,128]{2,1,0:T(8,128)}, u32[]{:S(2)}) copy-start(f32[12,16,128]{2,1,0:T(8,128)} %param.5) | copy-start | bytes 294916
  9.5 13.1 %collective-permute-start = (bf16[32,6,16,128]{3,2,1,0:T(8,128)(2,1)S(1)}, bf16[32,6,16,128]{3,2,1,0:T(8,128)(2,1)S(1)}, u32[]{:S(2)}, u32[]{:S(2)}) collective-permute-start(bf16[32,6,16,128]{3,2,1,0:T(8,128)(2,1)S(1)} %get-tuple-element.27), channel_id=1, source_target_pairs={{1,0},{2,1},{3,2},{4,3},{5,4},{6,5},{7,6},{8,7},{9,8},{10,9},{11,1... | collective-permute-start | bytes 2359304 | tf_op jit(solution)/shard_map/ppermute | solution.py:29
  13.2 15.4 %collective-permute-start.1 = (bf16[32,6,16,128]{3,2,1,0:T(8,128)(2,1)S(1)}, bf16[32,6,16,128]{3,2,1,0:T(8,128)(2,1)S(1)}, u32[]{:S(2)}, u32[]{:S(2)}) collective-permute-start(bf16[32,6,16,128]{3,2,1,0:T(8,128)(2,1)S(1)} %get-tuple-element.28), channel_id=1, source_target_pairs={{0,1},{1,2},{2,3},{3,4},{4,5},{5,6},{6,7},{7,8},{8,9},{9,10},{10,1... | collective-permute-start | bytes 2359304 | tf_op jit(solution)/shard_map/ppermute | solution.py:26
  56.8 11.4 %collective-permute-start.2 = (bf16[32,6,16,128]{3,2,1,0:T(8,128)(2,1)S(1)}, bf16[32,6,16,128]{3,2,1,0:T(8,128)(2,1)S(1)}, u32[]{:S(2)}, u32[]{:S(2)}) collective-permute-start(bf16[32,6,16,128]{3,2,1,0:T(8,128)(2,1)S(1)} %get-tuple-element.25), channel_id=1, source_target_pairs={{1,0},{2,1},{3,2},{4,3},{5,4},{6,5},{7,6},{8,7},{9,8},{10,9},{11,1... | collective-permute-start | bytes 2359304 | tf_op jit(solution)/shard_map/ppermute | solution.py:29
  58.7 24.3 %copy-start = (bf16[32,12,16,128]{3,2,1,0:T(8,128)(2,1)S(1)}, bf16[32,12,16,128]{3,2,1,0:T(8,128)(2,1)}, u32[]{:S(2)}) copy-start(bf16[32,12,16,128]{3,2,1,0:T(8,128)(2,1)} %param.3) | copy-start | bytes 4718596
  58.7 15.6 %collective-permute-start.3 = (bf16[32,6,16,128]{3,2,1,0:T(8,128)(2,1)S(1)}, bf16[32,6,16,128]{3,2,1,0:T(8,128)(2,1)S(1)}, u32[]{:S(2)}, u32[]{:S(2)}) collective-permute-start(bf16[32,6,16,128]{3,2,1,0:T(8,128)(2,1)S(1)} %get-tuple-element.26), channel_id=1, source_target_pairs={{0,1},{1,2},{2,3},{3,4},{4,5},{5,6},{6,7},{7,8},{8,9},{9,10},{10,1... | collective-permute-start | bytes 2359304 | tf_op jit(solution)/shard_map/ppermute | solution.py:26
  103.1 11.4 %collective-permute-start.4 = (bf16[32,6,16,128]{3,2,1,0:T(8,128)(2,1)S(1)}, bf16[32,6,16,128]{3,2,1,0:T(8,128)(2,1)S(1)}, u32[]{:S(2)}, u32[]{:S(2)}) collective-permute-start(bf16[32,6,16,128]{3,2,1,0:T(8,128)(2,1)S(1)} %get-tuple-element.23), channel_id=1, source_target_pairs={{1,0},{2,1},{3,2},{4,3},{5,4},{6,5},{7,6},{8,7},{9,8},{10,9},{11,1... | collective-permute-start | bytes 2359304 | tf_op jit(solution)/shard_map/ppermute | solution.py:29
  105.0 15.4 %collective-permute-start.5 = (bf16[32,6,16,128]{3,2,1,0:T(8,128)(2,1)S(1)}, bf16[32,6,16,128]{3,2,1,0:T(8,128)(2,1)S(1)}, u32[]{:S(2)}, u32[]{:S(2)}) collective-permute-start(bf16[32,6,16,128]{3,2,1,0:T(8,128)(2,1)S(1)} %get-tuple-element.24), channel_id=1, source_target_pairs={{0,1},{1,2},{2,3},{3,4},{4,5},{5,6},{6,7},{7,8},{8,9},{9,10},{10,1... | collective-permute-start | bytes 2359304 | tf_op jit(solution)/shard_map/ppermute | solution.py:26
Sparse Core Ops, SparseCore 0:
  186.8 257.9 all-reduce.5
where the time goes:
time: 567 us; the launch traced here: 560 us
  waiting for transfers between devices  298 us (53%)
  other arithmetic  143 us (25%)
  blocking collectives  77 us (14%)
  between operations  15 us (3%)
  starting transfers between devices  14.4 us (3%)
  local copies, waits for them, and re-layouts  9.96 us (2%)
    psum x1, waiting for transfers between devices, body(): gram_sum = lax.psum(partial_gram, ('band', 'domain'))  258 us
    all_to_all x1, blocking collectives, body(): lax.all_to_all(mixed, 'band', split_axis=0, concat_axis=1, tiled=True)  42 us
    all_to_all x1, blocking collectives, body(): lax.all_to_all(flattened, 'band', split_axis=1, concat_axis=0, tiled=True)  35 us
    another operation x6, other arithmetic, body(): lower_factor = jnp.linalg.cholesky(correlation)  34 us
    concatenate x3, other arithmetic, padded_2(): block = jnp.concatenate([low, block, high], axis=dim)  26.2 us
    ppermute x3, waiting for transfers between devices, padded_2(): lax.ppermute(lax.slice_in_dim(block, 0, width, axis=dim), axis, backward)  21.5 us
    another operation x3, other arithmetic, body(): jax.scipy.linalg.solve_triangular(lower_factor, jnp.eye(correlation.shape...  19.9 us
    convert_element_type x1, other arithmetic, body(): second = (2.0 * sigma_two / width_e * centred(extend(first_iter), potenti...  19.7 us
  transfers between devices with their start and end apart: 7, of which 7 were waited for; matrix products, arithmetic and copies ran while one was open for 0% of the time, Pallas kernels for 0%

commit v1 on v0

--- a/solution.py
+++ b/solution.py
@@ -1,7 +1,126 @@
+import functools
 import jax
 import jax.numpy as jnp
 from jax import lax
+from jax.experimental import pallas as pl
+from jax.experimental.pallas import tpu as pltpu
 from jax.sharding import PartitionSpec as P
+
+MESH = pl.DeviceIdType.MESH
+
+
+def remote(src, dst, send_sem, recv_sem, device):
+    return pltpu.make_async_remote_copy(
+        src_ref=src, dst_ref=dst, send_sem=send_sem, recv_sem=recv_sem,
+        device_id=device, device_id_type=MESH,
+    )
+
+
+def all_reduce_kernel(nx, ny, nzl, nzh, part_ref, out_ref, half, rows, line, mine,
+                      core_s, core_r, plane_s, plane_r, line_s, line_r, back_s, back_r, last_s, last_r):
+    band = lax.axis_index("band")
+    domain = lax.axis_index("domain")
+    y, z_hi = band // nzh, lax.rem(band, nzh)
+    core = lax.rem(domain, 2)
+    x = lax.rem(domain // 2, nx)
+    z_lo = domain // (2 * nx)
+    place = y * nx + x
+    planes = nx * ny
+    level = z_hi * nzl + z_lo
+    levels = nzl * nzh
+    size = part_ref.shape[0]
+    halfrows = size // 2
+    piece = halfrows // planes
+
+    partner = (band, domain + 1 - 2 * core)
+
+    def at_place(p):
+        return ((p // nx) * nzh + z_hi, (z_lo * nx + lax.rem(p, nx)) * 2 + core)
+
+    def at_level(l):
+        return (y * nzh + l // nzl, (lax.rem(l, nzl) * nx + x) * 2 + core)
+
+    barrier = pltpu.get_barrier_semaphore()
+    pl.semaphore_signal(barrier, inc=1, device_id=partner, device_id_type=MESH)
+    for k in range(1, planes):
+        pl.semaphore_signal(barrier, inc=1, device_id=at_place(lax.rem(place + k, planes)), device_id_type=MESH)
+    for k in range(1, levels):
+        pl.semaphore_signal(barrier, inc=1, device_id=at_level(lax.rem(level + k, levels)), device_id_type=MESH)
+    pl.semaphore_wait(barrier, planes + levels - 1)
+
+    mine_at = pl.multiple_of(core * halfrows, 8)
+    other_at = pl.multiple_of((1 - core) * halfrows, 8)
+    swap = remote(part_ref.at[pl.ds(other_at, halfrows)], half, core_s, core_r, partner)
+    swap.start()
+    swap.wait()
+    half[...] += part_ref[pl.ds(mine_at, halfrows), :]
+
+    copies = []
+    for k in range(1, planes):
+        p = lax.rem(place + k, planes)
+        copy = remote(half.at[pl.ds(pl.multiple_of(p * piece, 8), piece)], rows.at[place],
+                      plane_s.at[k], plane_r.at[k], at_place(p))
+        copy.start()
+        copies.append(copy)
+    rows[place] = half[pl.ds(pl.multiple_of(place * piece, 8), piece), :]
+    for copy in copies:
+        copy.wait()
+    total = rows[0]
+    for k in range(1, planes):
+        total = total + rows[k]
+    mine[...] = total
+
+    copies = []
+    for k in range(1, levels):
+        l = lax.rem(level + k, levels)
+        copy = remote(mine, line.at[level], line_s.at[k], line_r.at[k], at_level(l))
+        copy.start()
+        copies.append(copy)
+    line[level] = mine[...]
+    for copy in copies:
+        copy.wait()
+    total = line[0]
+    for k in range(1, levels):
+        total = total + line[k]
+    own = pl.ds(pl.multiple_of(mine_at + place * piece, 8), piece)
+    out_ref[own, :] = total
+
+    copies = []
+    for k in range(1, planes):
+        p = lax.rem(place + k, planes)
+        copy = remote(out_ref.at[own], out_ref.at[own], back_s.at[k], back_r.at[k], at_place(p))
+        copy.start()
+        copies.append(copy)
+    for copy in copies:
+        copy.wait()
+    span = pl.ds(mine_at, halfrows)
+    final = remote(out_ref.at[span], out_ref.at[span], last_s, last_r, partner)
+    final.start()
+    final.wait()
+
+
+def all_reduce(part, nx, ny, nzl, nzh, collective_id):
+    size, width = part.shape
+    planes, levels = nx * ny, nzl * nzh
+    piece = size // 2 // planes
+    dma = pltpu.SemaphoreType.DMA
+    f32 = jnp.float32
+    return pl.pallas_call(
+        functools.partial(all_reduce_kernel, nx, ny, nzl, nzh),
+        out_shape=jax.ShapeDtypeStruct((size, width), f32),
+        in_specs=[pl.BlockSpec(memory_space=pltpu.VMEM)],
+        out_specs=pl.BlockSpec(memory_space=pltpu.VMEM),
+        scratch_shapes=[
+            pltpu.VMEM((size // 2, width), f32),
+            pltpu.VMEM((planes, piece, width), f32),
+            pltpu.VMEM((levels, piece, width), f32),
+            pltpu.VMEM((piece, width), f32),
+            dma, dma, dma((planes,)), dma((planes,)), dma((levels,)), dma((levels,)),
+            dma((planes,)), dma((planes,)), dma, dma,
+        ],
+        compiler_params=pltpu.CompilerParams(collective_id=collective_id, has_side_effects=True),
+        name="correlation_sum",
+    )(part)
 
 grid_step = 0.5
 stencil_coef = (
@@ -99,7 +218,7 @@
     partial_gram = lax.dot_general(
         columns, columns, (((1,), (1,)), ((), ())), preferred_element_type=jnp.float32
     )
-    gram_sum = lax.psum(partial_gram, ("band", "domain"))
+    gram_sum = all_reduce(partial_gram, 4, 4, 4, 2, 1)
     correlation = gram_sum / float(cell_count * lax.axis_size("domain"))
     lower_factor = jnp.linalg.cholesky(correlation)
     inverse = jax.scipy.linalg.solve_triangular(

time: 567 us -> 331 us (0.58)
  waiting for transfers between devices: 298 us -> 64.5 us
  Pallas kernels: 0 us -> 35.4 us
  blocking collectives: 77 us -> 46.7 us
  between operations: 15 us -> 1.66 us
  starting transfers between devices: 14.4 us -> 24.6 us
    psum x1 -> x0, waiting for transfers between devices: 258 us -> none  [body(): gram_sum = lax.psum(partial_gram, ('band', 'domain'))]
    pallas_call x0 -> x1, Pallas kernels: none -> 35.4 us  [all_reduce(): pl.pallas_call(functools.partial(all_reduce_kernel, nx, ny, nzl, nzh), ou...]
    all_to_all x1 -> x0, blocking collectives: 35 us -> none  [body(): lax.all_to_all(flattened, 'band', split_axis=1, concat_axis=0, tiled=True)]
    all_to_all x0 -> x1, waiting for transfers between devices: none -> 25 us  [body(): lax.all_to_all(flattened, 'band', split_axis=1, concat_axis=0, tiled=True)]
    all_to_all x0 -> x1, starting transfers between devices: none -> 10.2 us  [body(): lax.all_to_all(flattened, 'band', split_axis=1, concat_axis=0, tiled=True)]
where the time goes in v1:
time: 331 us; the launch traced here: 329 us
  other arithmetic  141 us (43%)
  waiting for transfers between devices  64.5 us (19%)
  blocking collectives  46.7 us (14%)
  Pallas kernels  35.4 us (11%)
  starting transfers between devices  24.6 us (7%)
  local copies, waits for them, and re-layouts  12.1 us (4%)
    all_to_all x1, blocking collectives, body(): lax.all_to_all(mixed, 'band', split_axis=0, concat_axis=1, tiled=True)  46.7 us
    pallas_call x1, Pallas kernels, all_reduce(): pl.pallas_call(functools.partial(all_reduce_kernel, nx, ny, nzl, nzh), ou...  35.4 us
    another operation x6, other arithmetic, body(): lower_factor = jnp.linalg.cholesky(correlation)  34 us
    concatenate x3, other arithmetic, padded_2(): block = jnp.concatenate([low, block, high], axis=dim)  26.2 us
    all_to_all x1, waiting for transfers between devices, body(): lax.all_to_all(flattened, 'band', split_axis=1, concat_axis=0, tiled=True)  25 us
    ppermute x3, waiting for transfers between devices, padded_2(): lax.ppermute(lax.slice_in_dim(block, 0, width, axis=dim), axis, backward)  21.5 us
    another operation x3, other arithmetic, body(): jax.scipy.linalg.solve_triangular(lower_factor, jnp.eye(correlation.shape...  19.9 us
    convert_element_type x1, other arithmetic, body(): second = (2.0 * sigma_two / width_e * centred(extend(first_iter), potenti...  19.7 us
  transfers between devices with their start and end apart: 7, of which 7 were waited for; matrix products, arithmetic and copies ran while one was open for 0% of the time, Pallas kernels for 0%

profile of v1, /device:TPU:64, one launch (start us, length us, event | category | flops | bytes accessed | tf_op | source)
XLA Modules:
  0.0 328.9 jit_solution(1329693263210395519)
XLA Ops:
  0.8 1.9 multiply_convert_fusion
  3.0 3.7 %collective-permute-start = (bf16[32,6,16,128]{3,2,1,0:T(8,128)(2,1)S(1)}, bf16[32,6,16,128]{3,2,1,0:T(8,128)(2,1)S(1)}, u32[]{:S(2)}, u32[]{:S(2)}) collective-permute-start(bf16[32,6,16,128]{3,2,1,0:T(8,128)(2,1)S(1)} %get-tuple-element.27), channel_id=1, source_target_pairs={{1,0},{2,1},{3,2},{4,3},{5,4},{6,5},{7,6},{8,7},{9,8},{10,9},{11,1... | collective-permute-start | bytes 2359304 | tf_op jit(solution)/shard_map/ppermute | solution.py:148
  6.6 1.9 collective-permute-start.1
  8.6 7.5 %collective-permute-done = bf16[32,6,16,128]{3,2,1,0:T(8,128)(2,1)S(1)} collective-permute-done((bf16[32,6,16,128]{3,2,1,0:T(8,128)(2,1)S(1)}, bf16[32,6,16,128]{3,2,1,0:T(8,128)(2,1)S(1)}, u32[]{:S(2)}, u32[]{:S(2)}) %collective-permute-start) | collective-permute-done | bytes 786464 | tf_op jit(solution)/shard_map/ppermute | solution.py:148
  16.1 5.9 %collective-permute-done.1 = bf16[32,6,16,128]{3,2,1,0:T(8,128)(2,1)S(1)} collective-permute-done((bf16[32,6,16,128]{3,2,1,0:T(8,128)(2,1)S(1)}, bf16[32,6,16,128]{3,2,1,0:T(8,128)(2,1)S(1)}, u32[]{:S(2)}, u32[]{:S(2)}) %collective-permute-start.1) | collective-permute-done | bytes 786464 | tf_op jit(solution)/shard_map/ppermute | solution.py:145
  22.1 8.7 %select_maximum_fusion.4 = bf16[32,24,28,140]{3,2,1,0:T(8,128)(2,1)S(1)} fusion(bf16[32,6,16,128]{3,2,1,0:T(8,128)(2,1)S(1)} %collective-permute-done, bf16[32,12,16,128]{3,2,1,0:T(8,128)(2,1)S(1)} %multiply_convert_fusion, bf16[32,6,16,128]{3,2,1,0:T(8,128)(2,1)S(1)} %collective-permute-done.1), kind=kLoop, calls=%fused_computation.13 | loop fusion | flops 57200640 | bytes 9166848 | tf_op jit(solution)/shard_map/concatenate | solution.py:149
  30.8 19.2 %fusion.21 = bf16[32,12,16,128]{3,2,1,0:T(8,128)(2,1)S(1)} fusion(bf16[32,12,16,128]{3,2,1,0:T(8,128)(2,1)S(1)} %multiply_convert_fusion, bf16[32,6,16,128]{3,2,1,0:T(8,128)(2,1)S(1)} %collective-permute-done.1, bf16[32,6,16,128]{3,2,1,0:T(8,128)(2,1)S(1)} %collective-permute-done, bf16[32,24,28,140]{3,2,1,0:T(8,128)(2,1)S(1)} %select_maximum_fusion.4, ...), kind=kLoop, calls=%fused_computation.72 | loop fusion | flops 75497472 | bytes 42565632 | tf_op jit(solution)/shard_map/convert_element_type | solution.py:206
  50.2 1.9 collective-permute-start.2
  52.2 2.5 collective-permute-start.3
  54.7 6.9 %collective-permute-done.2 = bf16[32,6,16,128]{3,2,1,0:T(8,128)(2,1)S(1)} collective-permute-done((bf16[32,6,16,128]{3,2,1,0:T(8,128)(2,1)S(1)}, bf16[32,6,16,128]{3,2,1,0:T(8,128)(2,1)S(1)}, u32[]{:S(2)}, u32[]{:S(2)}) %collective-permute-start.2) | collective-permute-done | bytes 786464 | tf_op jit(solution)/shard_map/ppermute | solution.py:148
  61.7 6.1 %collective-permute-done.3 = bf16[32,6,16,128]{3,2,1,0:T(8,128)(2,1)S(1)} collective-permute-done((bf16[32,6,16,128]{3,2,1,0:T(8,128)(2,1)S(1)}, bf16[32,6,16,128]{3,2,1,0:T(8,128)(2,1)S(1)}, u32[]{:S(2)}, u32[]{:S(2)}) %collective-permute-start.3) | collective-permute-done | bytes 786464 | tf_op jit(solution)/shard_map/ppermute | solution.py:145
  67.7 8.7 %select_maximum_fusion.2 = bf16[32,24,28,140]{3,2,1,0:T(8,128)(2,1)S(1)} fusion(bf16[32,6,16,128]{3,2,1,0:T(8,128)(2,1)S(1)} %collective-permute-done.2, bf16[32,12,16,128]{3,2,1,0:T(8,128)(2,1)S(1)} %fusion.21, bf16[32,6,16,128]{3,2,1,0:T(8,128)(2,1)S(1)} %collective-permute-done.3), kind=kLoop, calls=%fused_computation.11 | loop fusion | flops 57200640 | bytes 9166848 | tf_op jit(solution)/shard_map/concatenate | solution.py:149
  76.5 19.7 %fusion.23 = bf16[32,12,16,128]{3,2,1,0:T(8,128)(2,1)S(1)} fusion(bf16[32,12,16,128]{3,2,1,0:T(8,128)(2,1)S(1)} %fusion.21, bf16[32,6,16,128]{3,2,1,0:T(8,128)(2,1)S(1)} %collective-permute-done.3, bf16[32,6,16,128]{3,2,1,0:T(8,128)(2,1)S(1)} %collective-permute-done.2, bf16[32,24,28,140]{3,2,1,0:T(8,128)(2,1)S(1)} %select_maximum_fusion.2, ...), kind=kLoop, calls=%fused_computation.74 | loop fusion | flops 80216064 | bytes 44140032 | tf_op jit(solution)/shard_map/convert_element_type | solution.py:210
  96.5 1.9 collective-permute-start.4
  98.4 2.4 collective-permute-start.5
  100.9 7.1 %collective-permute-done.4 = bf16[32,6,16,128]{3,2,1,0:T(8,128)(2,1)S(1)} collective-permute-done((bf16[32,6,16,128]{3,2,1,0:T(8,128)(2,1)S(1)}, bf16[32,6,16,128]{3,2,1,0:T(8,128)(2,1)S(1)}, u32[]{:S(2)}, u32[]{:S(2)}) %collective-permute-start.4) | collective-permute-done | bytes 786464 | tf_op jit(solution)/shard_map/ppermute | solution.py:148
  107.9 5.9 %collective-permute-done.5 = bf16[32,6,16,128]{3,2,1,0:T(8,128)(2,1)S(1)} collective-permute-done((bf16[32,6,16,128]{3,2,1,0:T(8,128)(2,1)S(1)}, bf16[32,6,16,128]{3,2,1,0:T(8,128)(2,1)S(1)}, u32[]{:S(2)}, u32[]{:S(2)}) %collective-permute-start.5) | collective-permute-done | bytes 786464 | tf_op jit(solution)/shard_map/ppermute | solution.py:145
  113.9 8.7 %select_maximum_fusion = bf16[32,24,28,140]{3,2,1,0:T(8,128)(2,1)S(1)} fusion(bf16[32,6,16,128]{3,2,1,0:T(8,128)(2,1)S(1)} %collective-permute-done.4, bf16[32,12,16,128]{3,2,1,0:T(8,128)(2,1)S(1)} %fusion.23, bf16[32,6,16,128]{3,2,1,0:T(8,128)(2,1)S(1)} %collective-permute-done.5), kind=kLoop, calls=%fused_computation.9 | loop fusion | flops 57200640 | bytes 9166848 | tf_op jit(solution)/shard_map/concatenate | solution.py:149
  122.6 19.6 %fusion.12 = bf16[32,12,16,128]{3,2,1,0:T(8,128)(2,1)S(1)} fusion(bf16[32,12,16,128]{3,2,1,0:T(8,128)(2,1)S(1)} %fusion.23, bf16[32,12,16,128]{3,2,1,0:T(8,128)(2,1)S(1)} %fusion.21, bf16[32,6,16,128]{3,2,1,0:T(8,128)(2,1)S(1)} %collective-permute-done.5, bf16[32,6,16,128]{3,2,1,0:T(8,128)(2,1)S(1)} %collective-permute-done.4, ...), kind=kLoop, calls=%fused_computation.63 | loop fusion | flops 77856768 | bytes 44138496 | tf_op jit(solution)/shard_map/convert_element_type | solution.py:214
  142.9 2.0 copy.18
  144.9 10.2 %all-to-all-start = ((bf16[32,8,3072]{2,0,1:T(8,128)(2,1)}), bf16[32,8,3072]{2,0,1:T(8,128)(2,1)S(1)}, u32[]{:S(2)}, u32[]{:S(2)}) async-start(bf16[32,8,3072]{2,0,1:T(8,128)(2,1)} %copy.18), calls=%async_computation | async-start | bytes 3145728 | tf_op jit(solution)/shard_map/all_to_all | solution.py:217
  155.2 25.0 %all-to-all-done = bf16[32,8,3072]{2,0,1:T(8,128)(2,1)S(1)} async-done(((bf16[32,8,3072]{2,0,1:T(8,128)(2,1)}), bf16[32,8,3072]{2,0,1:T(8,128)(2,1)S(1)}, u32[]{:S(2)}, u32[]{:S(2)}) %all-to-all-start) | async-done | bytes 1572896 | tf_op jit(solution)/shard_map/all_to_all | solution.py:217
  181.5 35.4 %correlation_sum.1 = f32[256,256]{1,0:T(8,128)} custom-call(f32[256,256]{1,0:T(8,128)} %fusion.78.part_ref), custom_call_target="tpu_custom_call" | custom-call | tf_op jit(solution)/shard_map/correlation_sum/pallas_call | solution.py:108
  218.3 11.7 %cholesky.50 = f32[128,128]{1,0:T(8,128)S(1)} custom-call(f32[128,128]{1,0:T(8,128)S(1)} %cholesky.118), custom_call_target="Cholesky" | custom-call | tf_op jit(solution)/shard_map/jit(cholesky)/cholesky | solution.py:223
  230.0 9.8 %custom-call.15 = f32[1,128,128]{1,2,0:T(8,128)S(1)} custom-call(f32[1,128,128]{2,1,0:T(8,128)S(1)} %get-tuple-element.32), custom_call_target="InvertDiagBlocksLowerTriangular" | custom-call | tf_op jit(solution)/shard_map/jit(cholesky)/cholesky | solution.py:223
  240.3 11.7 %cholesky.105 = f32[128,128]{1,0:T(8,128)S(1)} custom-call(f32[128,128]{1,0:T(8,128)S(1)} %convolution_subtract_fusion.1), custom_call_target="Cholesky" | custom-call | tf_op jit(solution)/shard_map/jit(cholesky)/cholesky | solution.py:223
  254.2 4.1 %while.1 = (s32[]{:T(128)}, f32[256,256]{1,0:T(8,128)S(1)}, s32[2,2]{1,0:T(2,128)S(1)}, f32[2,128,128]{2,1,0:T(8,128)S(1)}, s32[]{:T(128)}) while((s32[]{:T(128)}, f32[256,256]{1,0:T(8,128)S(1)}, s32[2,2]{1,0:T(2,128)S(1)}, f32[2,128,128]{2,1,0:T(8,128)S(1)}, s32[]{:T(128)}) %tuple.27), condition=%wide.while_cond, body=%wide.while_body.sunk | while | flops 2 | bytes 131181 | solution.py:224
  254.8 1.4 bitcast_dynamic-update-slice_fusion.2
  256.9 1.4 bitcast_dynamic-update-slice_fusion.2
  258.3 19.9 %custom-call.16 = f32[2,128,128]{1,2,0:T(8,128)S(1)} custom-call(f32[2,128,128]{2,1,0:T(8,128)S(1)} %get-tuple-element.12), custom_call_target="InvertDiagBlocksLowerTriangular" | custom-call | tf_op jit(solution)/shard_map/jit(_solve_triangular)/triangular_solve | solution.py:224
  279.7 46.7 %all_to_all.35 = bf16[8,32,3072]{2,1,0:T(8,128)(2,1)S(1)} all-to-all(bf16[8,32,3072]{2,1,0:T(8,128)(2,1)S(1)} %bitcast.45), channel_id=1, replica_groups=mesh['band'=8,'domain'=32] {'band'}, dimensions={0} | all-to-all | bytes 3145728 | tf_op jit(solution)/shard_map/all_to_all | solution.py:229
  327.3 1.6 reshape.34
  (36 shorter events, 9.8 us)
Async XLA Ops:
  0.8 7.8 %copy-start.1 = (f32[12,16,128]{2,1,0:T(8,128)S(1)}, f32[12,16,128]{2,1,0:T(8,128)}, u32[]{:S(2)}) copy-start(f32[12,16,128]{2,1,0:T(8,128)} %param.5) | copy-start | bytes 294916
  3.0 13.1 %collective-permute-start = (bf16[32,6,16,128]{3,2,1,0:T(8,128)(2,1)S(1)}, bf16[32,6,16,128]{3,2,1,0:T(8,128)(2,1)S(1)}, u32[]{:S(2)}, u32[]{:S(2)}) collective-permute-start(bf16[32,6,16,128]{3,2,1,0:T(8,128)(2,1)S(1)} %get-tuple-element.27), channel_id=1, source_target_pairs={{1,0},{2,1},{3,2},{4,3},{5,4},{6,5},{7,6},{8,7},{9,8},{10,9},{11,1... | collective-permute-start | bytes 2359304 | tf_op jit(solution)/shard_map/ppermute | solution.py:148
  6.6 15.4 %collective-permute-start.1 = (bf16[32,6,16,128]{3,2,1,0:T(8,128)(2,1)S(1)}, bf16[32,6,16,128]{3,2,1,0:T(8,128)(2,1)S(1)}, u32[]{:S(2)}, u32[]{:S(2)}) collective-permute-start(bf16[32,6,16,128]{3,2,1,0:T(8,128)(2,1)S(1)} %get-tuple-element.28), channel_id=1, source_target_pairs={{0,1},{1,2},{2,3},{3,4},{4,5},{5,6},{6,7},{7,8},{8,9},{9,10},{10,1... | collective-permute-start | bytes 2359304 | tf_op jit(solution)/shard_map/ppermute | solution.py:145
  50.2 11.4 %collective-permute-start.2 = (bf16[32,6,16,128]{3,2,1,0:T(8,128)(2,1)S(1)}, bf16[32,6,16,128]{3,2,1,0:T(8,128)(2,1)S(1)}, u32[]{:S(2)}, u32[]{:S(2)}) collective-permute-start(bf16[32,6,16,128]{3,2,1,0:T(8,128)(2,1)S(1)} %get-tuple-element.25), channel_id=1, source_target_pairs={{1,0},{2,1},{3,2},{4,3},{5,4},{6,5},{7,6},{8,7},{9,8},{10,9},{11,1... | collective-permute-start | bytes 2359304 | tf_op jit(solution)/shard_map/ppermute | solution.py:148
  52.2 24.3 %copy-start = (bf16[32,12,16,128]{3,2,1,0:T(8,128)(2,1)S(1)}, bf16[32,12,16,128]{3,2,1,0:T(8,128)(2,1)}, u32[]{:S(2)}) copy-start(bf16[32,12,16,128]{3,2,1,0:T(8,128)(2,1)} %param.3) | copy-start | bytes 4718596
  52.2 15.6 %collective-permute-start.3 = (bf16[32,6,16,128]{3,2,1,0:T(8,128)(2,1)S(1)}, bf16[32,6,16,128]{3,2,1,0:T(8,128)(2,1)S(1)}, u32[]{:S(2)}, u32[]{:S(2)}) collective-permute-start(bf16[32,6,16,128]{3,2,1,0:T(8,128)(2,1)S(1)} %get-tuple-element.26), channel_id=1, source_target_pairs={{0,1},{1,2},{2,3},{3,4},{4,5},{5,6},{6,7},{7,8},{8,9},{9,10},{10,1... | collective-permute-start | bytes 2359304 | tf_op jit(solution)/shard_map/ppermute | solution.py:145
  96.5 11.4 %collective-permute-start.4 = (bf16[32,6,16,128]{3,2,1,0:T(8,128)(2,1)S(1)}, bf16[32,6,16,128]{3,2,1,0:T(8,128)(2,1)S(1)}, u32[]{:S(2)}, u32[]{:S(2)}) collective-permute-start(bf16[32,6,16,128]{3,2,1,0:T(8,128)(2,1)S(1)} %get-tuple-element.23), channel_id=1, source_target_pairs={{1,0},{2,1},{3,2},{4,3},{5,4},{6,5},{7,6},{8,7},{9,8},{10,9},{11,1... | collective-permute-start | bytes 2359304 | tf_op jit(solution)/shard_map/ppermute | solution.py:148
  98.4 15.4 %collective-permute-start.5 = (bf16[32,6,16,128]{3,2,1,0:T(8,128)(2,1)S(1)}, bf16[32,6,16,128]{3,2,1,0:T(8,128)(2,1)S(1)}, u32[]{:S(2)}, u32[]{:S(2)}) collective-permute-start(bf16[32,6,16,128]{3,2,1,0:T(8,128)(2,1)S(1)} %get-tuple-element.24), channel_id=1, source_target_pairs={{0,1},{1,2},{2,3},{3,4},{4,5},{5,6},{6,7},{7,8},{8,9},{9,10},{10,1... | collective-permute-start | bytes 2359304 | tf_op jit(solution)/shard_map/ppermute | solution.py:145
  144.9 35.3 %all-to-all-start = ((bf16[32,8,3072]{2,0,1:T(8,128)(2,1)}), bf16[32,8,3072]{2,0,1:T(8,128)(2,1)S(1)}, u32[]{:S(2)}, u32[]{:S(2)}) async-start(bf16[32,8,3072]{2,0,1:T(8,128)(2,1)} %copy.18), calls=%async_computation | async-start | bytes 3145728 | tf_op jit(solution)/shard_map/all_to_all | solution.py:217

commit v2 on v1

v2 whole, which is shorter than its diff:
```python
import functools

import jax
import jax.numpy as jnp
import ml_dtypes
import numpy as np
from jax import lax
from jax.experimental import pallas as pl
from jax.experimental.pallas import tpu as pltpu
from jax.sharding import PartitionSpec as P

MESH = pl.DeviceIdType.MESH

grid_step = 0.5
stencil_coef = (
    -5369.0 / 1800.0,
    12.0 / 7.0,
    -15.0 / 56.0,
    10.0 / 189.0,
    -1.0 / 112.0,
    2.0 / 1925.0,
    -1.0 / 16632.0,
)
lower_end = -4.0
cut_energy = 6.0
upper_end = 43.0


def filter_terms():
    width_e = (upper_end - cut_energy) / 2.0
    centre = (upper_end + cut_energy) / 2.0
    sigma_one = width_e / (lower_end - centre)
    gamma_term = 2.0 / sigma_one
    sigma_two = 1.0 / (gamma_term - sigma_one)
    sigma_three = 1.0 / (gamma_term - sigma_two)
    return (width_e, centre, sigma_one, sigma_two, sigma_three)


def remote(src, dst, send_sem, recv_sem, device):
    return pltpu.make_async_remote_copy(
        src_ref=src, dst_ref=dst, send_sem=send_sem, recv_sem=recv_sem,
        device_id=device, device_id_type=MESH,
    )


def all_reduce_kernel(nx, ny, nzl, nzh, part_ref, out_ref, half, rows, line, mine,
                      core_s, core_r, plane_s, plane_r, line_s, line_r, back_s, back_r, last_s, last_r):
    band = lax.axis_index("band")
    domain = lax.axis_index("domain")
    y, z_hi = band // nzh, lax.rem(band, nzh)
    core = lax.rem(domain, 2)
    x = lax.rem(domain // 2, nx)
    z_lo = domain // (2 * nx)
    place = y * nx + x
    planes = nx * ny
    level = z_hi * nzl + z_lo
    levels = nzl * nzh
    size = part_ref.shape[0]
    halfrows = size // 2
    piece = halfrows // planes

    partner = (band, domain + 1 - 2 * core)

    def at_place(p):
        return ((p // nx) * nzh + z_hi, (z_lo * nx + lax.rem(p, nx)) * 2 + core)

    def at_level(l):
        return (y * nzh + l // nzl, (lax.rem(l, nzl) * nx + x) * 2 + core)

    barrier = pltpu.get_barrier_semaphore()
    pl.semaphore_signal(barrier, inc=1, device_id=partner, device_id_type=MESH)
    for k in range(1, planes):
        pl.semaphore_signal(barrier, inc=1, device_id=at_place(lax.rem(place + k, planes)), device_id_type=MESH)
    for k in range(1, levels):
        pl.semaphore_signal(barrier, inc=1, device_id=at_level(lax.rem(level + k, levels)), device_id_type=MESH)
    pl.semaphore_wait(barrier, planes + levels - 1)

    mine_at = pl.multiple_of(core * halfrows, 8)
    other_at = pl.multiple_of((1 - core) * halfrows, 8)
    swap = remote(part_ref.at[pl.ds(other_at, halfrows)], half, core_s, core_r, partner)
    swap.start()
    swap.wait()
    half[...] += part_ref[pl.ds(mine_at, halfrows), :]

    copies = []
    for k in range(1, planes):
        p = lax.rem(place + k, planes)
        copy = remote(half.at[pl.ds(pl.multiple_of(p * piece, 8), piece)], rows.at[place],
                      plane_s.at[k], plane_r.at[k], at_place(p))
        copy.start()
        copies.append(copy)
    rows[place] = half[pl.ds(pl.multiple_of(place * piece, 8), piece), :]
    for copy in copies:
        copy.wait()
    total = rows[0]
    for k in range(1, planes):
        total = total + rows[k]
    mine[...] = total

    copies = []
    for k in range(1, levels):
        l = lax.rem(level + k, levels)
        copy = remote(mine, line.at[level], line_s.at[k], line_r.at[k], at_level(l))
        copy.start()
        copies.append(copy)
    line[level] = mine[...]
    for copy in copies:
        copy.wait()
    total = line[0]
    for k in range(1, levels):
        total = total + line[k]
    own = pl.ds(pl.multiple_of(mine_at + place * piece, 8), piece)
    out_ref[own, :] = total

    copies = []
    for k in range(1, planes):
        p = lax.rem(place + k, planes)
        copy = remote(out_ref.at[own], out_ref.at[own], back_s.at[k], back_r.at[k], at_place(p))
        copy.start()
        copies.append(copy)
    for copy in copies:
        copy.wait()
    span = pl.ds(mine_at, halfrows)
    final = remote(out_ref.at[span], out_ref.at[span], last_s, last_r, partner)
    final.start()
    final.wait()


def all_reduce(part, nx, ny, nzl, nzh, collective_id):
    size, width = part.shape
    planes, levels = nx * ny, nzl * nzh
    piece = size // 2 // planes
    dma = pltpu.SemaphoreType.DMA
    f32 = jnp.float32
    return pl.pallas_call(
        functools.partial(all_reduce_kernel, nx, ny, nzl, nzh),
        out_shape=jax.ShapeDtypeStruct((size, width), f32),
        in_specs=[pl.BlockSpec(memory_space=pltpu.VMEM)],
        out_specs=pl.BlockSpec(memory_space=pltpu.VMEM),
        scratch_shapes=[
            pltpu.VMEM((size // 2, width), f32),
            pltpu.VMEM((planes, piece, width), f32),
            pltpu.VMEM((levels, piece, width), f32),
            pltpu.VMEM((piece, width), f32),
            dma, dma, dma((planes,)), dma((planes,)), dma((levels,)), dma((levels,)),
            dma((planes,)), dma((planes,)), dma, dma,
        ],
        compiler_params=pltpu.CompilerParams(collective_id=collective_id, has_side_effects=True),
        name="correlation_sum",
    )(part)


def rotation_kernel(panel, cells, gram_ref, out_ref, work):
    size = gram_ref.shape[0]
    work[...] = gram_ref[...] * (1.0 / cells)
    lane = lax.broadcasted_iota(jnp.int32, (panel, size), 1)
    row = lax.broadcasted_iota(jnp.int32, (panel, size), 0)
    sub = lax.broadcasted_iota(jnp.int32, (panel, 128), 0)
    wide = lax.broadcasted_iota(jnp.int32, (size, size), 1)

    def step(k, carry):
        start = pl.multiple_of(k * panel, panel)
        tile = pl.multiple_of((start // 128) * 128, 128)
        here = pl.ds(start, panel)
        corner = pltpu.roll(work[here, pl.ds(tile, 128)], 128 - (start - tile), 1)
        rows = work[here, :]
        inside = (lane >= start) & (lane < start + panel)
        rows = jnp.where(inside, jnp.where(lane - start == row, 1.0, 0.0), rows)
        columns = [jnp.broadcast_to(corner[:, j : j + 1], (panel, 128)) for j in range(panel)]
        pivots = jnp.ones((panel, 128), jnp.float32)
        for j in range(panel):
            column = columns[j]
            spread = [jnp.broadcast_to(column[l : l + 1, :], (panel, 128)) for l in range(j, panel)]
            pivot = spread[0]
            pivots = jnp.where(sub == j, pivot, pivots)
            if j < panel - 1:
                factor = jnp.where(sub > j, column * (1.0 / pivot), 0.0)
                for l in range(j + 1, panel):
                    columns[l] = columns[l] - factor * spread[l - j]
                wide_factor = jnp.concatenate([factor] * (size // 128), axis=1)
                rows = rows - wide_factor * jnp.broadcast_to(rows[j : j + 1, :], (panel, size))
        scale = lax.rsqrt(pivots)
        rows = rows * jnp.concatenate([scale] * (size // 128), axis=1)
        below = jnp.where(lane >= start + panel, rows, 0.0)
        change = lax.dot_general(
            below, rows, (((0,), (0,)), ((), ())),
            precision=lax.Precision.HIGHEST, preferred_element_type=jnp.float32,
        )
        keep = (wide >= start) & (wide < start + panel)
        work[...] = jnp.where(keep, 0.0, work[...]) - change
        work[here, :] = rows
        return carry

    lax.fori_loop(0, size // panel, step, 0)
    down = lax.broadcasted_iota(jnp.int32, (size, size), 0)
    out_ref[...] = jnp.where(wide <= down, work[...], 0.0).astype(out_ref.dtype)


def rotation_of(gram, cells, panel=16):
    size = gram.shape[0]
    return pl.pallas_call(
        functools.partial(rotation_kernel, panel, cells),
        out_shape=jax.ShapeDtypeStruct((size, size), jnp.bfloat16),
        in_specs=[pl.BlockSpec(memory_space=pltpu.VMEM)],
        out_specs=pl.BlockSpec(memory_space=pltpu.VMEM),
        scratch_shapes=[pltpu.VMEM((size, size), jnp.float32)],
        name="rotation",
    )(gram)


def stencil_matrices(planes, rows_y, rows_z):
    reach = len(stencil_coef) - 1
    kinetic = -0.5 / (grid_step * grid_step)
    plane_part = np.zeros((planes, rows_y, planes + 2 * reach, rows_y), np.float64)
    line_part = np.zeros((rows_z, rows_z), np.float64)
    for m in range(1, reach + 1):
        weight = kinetic * stencil_coef[m]
        for sign in (-m, m):
            for x in range(planes):
                for y in range(rows_y):
                    plane_part[x, y, x + reach + sign, y] += weight
                    if 0 <= y + sign < rows_y:
                        plane_part[x, y, x + reach, y + sign] += weight
            for z in range(rows_z):
                if 0 <= z + sign < rows_z:
                    line_part[z + sign, z] += weight
    plane_part = plane_part.reshape(planes * rows_y, (planes + 2 * reach) * rows_y)

    def halves(matrix):
        high = matrix.astype(ml_dtypes.bfloat16)
        low = (matrix - high.astype(np.float64)).astype(ml_dtypes.bfloat16)
        return np.concatenate([high, low], axis=0)

    return halves(plane_part), halves(line_part)


GROUP = 8
SHARE = 16


def filter_kernel(
    nb, nd, orb_ref, scale_ref, pot_ref, plane_ref, line_ref, cols_ref, gram_ref,
    ext0, ext1, ext2, full, turned, energy,
    up_s, up_r, down_s, down_r, share_s, share_r,
):
    band = lax.axis_index("band")
    domain = lax.axis_index("domain")
    orbitals, planes, rows_y, rows_z = orb_ref.shape
    reach = len(stencil_coef) - 1
    cells_xy = planes * rows_y
    part = cells_xy // nb
    groups = orbitals // GROUP
    ext = (ext0, ext1, ext2)
    has_low, has_high = domain > 0, domain < nd - 1
    width_e, centre, sigma_one, sigma_two, sigma_three = filter_terms()
    kinetic = -0.5 / (grid_step * grid_step)

    barrier = pltpu.get_barrier_semaphore()

    @pl.when(has_low)
    def _():
        pl.semaphore_signal(barrier, inc=1, device_id=(band, domain - 1), device_id_type=MESH)

    @pl.when(has_high)
    def _():
        pl.semaphore_signal(barrier, inc=1, device_id=(band, domain + 1), device_id_type=MESH)

    for k in range(1, nb):
        pl.semaphore_signal(barrier, inc=1, device_id=(lax.rem(band + k, nb), domain), device_id_type=MESH)

    def scale_group(g):
        def one(i, carry):
            o = g * GROUP + i
            for p in range(planes):
                ext0[o, reach + p] = (orb_ref[o, p].astype(jnp.float32) * scale_ref[o, p]).astype(jnp.bfloat16)
            return carry

        lax.fori_loop(0, GROUP, one, 0)

    def upward(s, g):
        some = pl.ds(g * GROUP, GROUP)
        return remote(ext[s].at[some, pl.ds(planes, reach)], ext[s].at[some, pl.ds(0, reach)],
                      up_s.at[s, g], up_r.at[s, g], (band, domain + 1))

    def downward(s, g):
        some = pl.ds(g * GROUP, GROUP)
        return remote(ext[s].at[some, pl.ds(reach, reach)], ext[s].at[some, pl.ds(planes + reach, reach)],
                      down_s.at[s, g], down_r.at[s, g], (band, domain - 1))

    def send_edges(s, g):
        @pl.when(has_high)
        def _():
            upward(s, g).start()

        @pl.when(has_low)
        def _():
            downward(s, g).start()

    def await_edges(s, g):
        @pl.when(has_low)
        def _():
            upward(s, g).wait_recv()

        @pl.when(has_high)
        def _():
            downward(s, g).wait_recv()

    def apply(s, g):
        def pair(i, carry):
            o = g * GROUP + 2 * i
            sources = [ext[s][o + q].reshape((planes + 2 * reach) * rows_y, rows_z) for q in range(2)]
            both = jnp.concatenate(sources, axis=1)
            spread = jnp.dot(plane_ref[...], both, preferred_element_type=jnp.float32)
            spread = spread[:cells_xy] + spread[cells_xy:]
            first_row = reach * rows_y
            for q in range(2):
                middle = sources[q][first_row : first_row + cells_xy]
                along = jnp.dot(
                    jnp.concatenate([middle, middle], axis=1), line_ref[...], preferred_element_type=jnp.float32
                )
                total = spread[:, q * rows_z : (q + 1) * rows_z] + along + energy[...] * middle.astype(jnp.float32)
                if s == 0:
                    value = total * (sigma_one / width_e)
                else:
                    earlier = ext[s - 1][o + q, pl.ds(reach, planes)].reshape(cells_xy, rows_z).astype(jnp.float32)
                    if s == 1:
                        value = total * (2.0 * sigma_two / width_e) - (sigma_one * sigma_two) * earlier
                    else:
                        value = total * (2.0 * sigma_three / width_e) - (sigma_two * sigma_three) * earlier
                if s < 2:
                    ext[s + 1][o + q, pl.ds(reach, planes)] = value.astype(jnp.bfloat16).reshape(planes, rows_y, rows_z)
                else:
                    full[lax.rem(o, SHARE) + q] = value
            return carry

        lax.fori_loop(0, GROUP // 2, pair, 0)

    def turn(h):
        def block(r, carry):
            at = pl.multiple_of(r * 8, 8)
            piece = full[:, pl.ds(at, 8), :]
            turned[pl.ds(at, 8), pl.ds(h * SHARE, SHARE), :] = jnp.swapaxes(piece, 0, 1).astype(jnp.bfloat16)
            return carry

        lax.fori_loop(0, cells_xy // 8, block, 0)

    def place_of(b, h):
        return pl.ds(pl.multiple_of(b * orbitals + h * SHARE, SHARE), SHARE)

    def share(h, k):
        target = lax.rem(band + k, nb)
        return remote(turned.at[pl.ds(target * part, part), pl.ds(h * SHARE, SHARE)],
                      cols_ref.at[:, place_of(band, h)],
                      share_s.at[h, k], share_r.at[h, k], (target, domain))

    energy[...] = pot_ref[...].reshape(cells_xy, rows_z) + (3.0 * stencil_coef[0] * kinetic - centre)
    scale_group(0)
    pl.semaphore_wait(barrier, nb - 1 + has_low.astype(jnp.int32) + has_high.astype(jnp.int32))

    send_edges(0, 0)
    for g in range(1, groups):
        scale_group(g)
        send_edges(0, g)

    @pl.when(jnp.logical_not(has_low))
    def _():
        for s in range(3):
            ext[s][:, :reach] = jnp.zeros((orbitals, reach, rows_y, rows_z), jnp.bfloat16)

    @pl.when(jnp.logical_not(has_high))
    def _():
        for s in range(3):
            ext[s][:, planes + reach :] = jnp.zeros((orbitals, reach, rows_y, rows_z), jnp.bfloat16)

    for s, g in ((0, 0), (0, 1), (1, 0), (1, 1), (0, 2), (2, 0), (2, 1), (0, 3), (1, 2), (1, 3), (2, 2), (2, 3)):
        await_edges(s, g)
        apply(s, g)
        if s < 2:
            send_edges(s + 1, g)
        elif g % 2 == 1:
            h = g // 2
            turn(h)
            for k in range(1, nb):
                share(h, k).start()
            cols_ref[:, place_of(band, h), :] = turned[pl.ds(band * part, part), pl.ds(h * SHARE, SHARE), :]

    for h in range(orbitals // SHARE):
        for k in range(1, nb):
            share(h, k).wait()

    def gram_step(i, total):
        line = jnp.concatenate([cols_ref[2 * i], cols_ref[2 * i + 1]], axis=1)
        return total + lax.dot_general(line, line, (((1,), (1,)), ((), ())), preferred_element_type=jnp.float32)

    gram_ref[...] = lax.fori_loop(0, part // 2, gram_step, jnp.zeros(gram_ref.shape, jnp.float32))

    for s in range(3):
        for g in range(groups):
            @pl.when(has_high)
            def _():
                upward(s, g).wait_send()

            @pl.when(has_low)
            def _():
                downward(s, g).wait_send()


def filtered_columns(orbital_block, block_scale, potential, nb, nd, collective_id):
    orbitals, planes, rows_y, rows_z = orbital_block.shape
    reach = len(stencil_coef) - 1
    plane_part, line_part = stencil_matrices(planes, rows_y, rows_z)
    cells_xy = planes * rows_y
    groups = orbitals // GROUP
    halves = orbitals // SHARE
    dma = pltpu.SemaphoreType.DMA
    f32, bf16 = jnp.float32, jnp.bfloat16
    vmem = pl.BlockSpec(memory_space=pltpu.VMEM)
    wide = pltpu.VMEM((orbitals, planes + 2 * reach, rows_y, rows_z), bf16)
    return pl.pallas_call(
        functools.partial(filter_kernel, nb, nd),
        out_shape=(
            jax.ShapeDtypeStruct((cells_xy // nb, nb * orbitals, rows_z), bf16),
            jax.ShapeDtypeStruct((nb * orbitals, nb * orbitals), f32),
        ),
        in_specs=[vmem, pl.BlockSpec(memory_space=pltpu.SMEM), vmem, vmem, vmem],
        out_specs=(vmem, vmem),
        scratch_shapes=[
            wide, wide, wide,
            pltpu.VMEM((SHARE, cells_xy, rows_z), f32),
            pltpu.VMEM((cells_xy, orbitals, rows_z), bf16),
            pltpu.VMEM((cells_xy, rows_z), f32),
            dma((3, groups)), dma((3, groups)), dma((3, groups)), dma((3, groups)),
            dma((halves, nb)), dma((halves, nb)),
        ],
        compiler_params=pltpu.CompilerParams(collective_id=collective_id, has_side_effects=True, vmem_limit_bytes=48 << 20),
        name="filter",
    )(orbital_block, block_scale, potential, jnp.asarray(plane_part), jnp.asarray(line_part))


def rotate_kernel(nb, rot_ref, cols_ref, out_ref, mixed, send, recv):
    band = lax.axis_index("band")
    domain = lax.axis_index("domain")
    part, total, rows_z = cols_ref.shape
    orbitals = total // nb
    barrier = pltpu.get_barrier_semaphore()
    for k in range(1, nb):
        pl.semaphore_signal(barrier, inc=1, device_id=(lax.rem(band + k, nb), domain), device_id_type=MESH)

    chunks = send.shape[0]
    span = part // chunks

    def back(c, k):
        target = lax.rem(band + k, nb)
        rows = pl.ds(pl.multiple_of(target * orbitals, orbitals), orbitals)
        return remote(mixed.at[pl.ds(c * span, span), rows],
                      out_ref.at[pl.ds(band * part + c * span, span)],
                      send.at[c, k], recv.at[c, k], (target, domain))

    for c in range(chunks):
        def mix(i, carry):
            r = c * span + 2 * i
            line = jnp.concatenate([cols_ref[r], cols_ref[r + 1]], axis=1)
            value = jnp.dot(rot_ref[...], line, preferred_element_type=jnp.float32).astype(jnp.bfloat16)
            mixed[r] = value[:, :rows_z]
            mixed[r + 1] = value[:, rows_z:]
            return carry

        lax.fori_loop(0, span // 2, mix, 0)
        if c == 0:
            pl.semaphore_wait(barrier, nb - 1)
        for k in range(1, nb):
            back(c, k).start()

    own = pl.ds(pl.multiple_of(band * orbitals, orbitals), orbitals)
    out_ref[pl.ds(band * part, part)] = mixed[:, own, :]
    for c in range(chunks):
        for k in range(1, nb):
            back(c, k).wait()


def rotated(rotation, columns, nb, collective_id, chunks=4):
    part, total, rows_z = columns.shape
    orbitals = total // nb
    dma = pltpu.SemaphoreType.DMA
    vmem = pl.BlockSpec(memory_space=pltpu.VMEM)
    return pl.pallas_call(
        functools.partial(rotate_kernel, nb),
        out_shape=jax.ShapeDtypeStruct((part * nb, orbitals, rows_z), jnp.bfloat16),
        in_specs=[vmem, vmem],
        out_specs=vmem,
        scratch_shapes=[pltpu.VMEM((part, total, rows_z), jnp.bfloat16), dma((chunks, nb)), dma((chunks, nb))],
        compiler_params=pltpu.CompilerParams(collective_id=collective_id, has_side_effects=True, vmem_limit_bytes=48 << 20),
        name="rotate",
    )(rotation, columns)


def solution(mesh):
    nb, nd = mesh.shape["band"], mesh.shape["domain"]

    def body(orbital_block, block_scale, potential):
        orbitals, planes, rows_y, rows_z = orbital_block.shape
        columns, part = filtered_columns(orbital_block, block_scale, potential, nb, nd, 1)
        gram = all_reduce(part, 4, 4, 4, 2, 2)
        rotation = rotation_of(gram, float(planes * rows_y * rows_z * nd), 32)
        back = rotated(rotation, columns, nb, 3)
        return back.transpose(1, 0, 2).reshape(orbitals, planes, rows_y, rows_z)

    in_specs = (P("band", "domain", None, None), P("band", "domain"), P("domain", None, None))
    out_specs = P("band", "domain", None, None)
    return jax.shard_map(body, mesh=mesh, in_specs=in_specs, out_specs=out_specs, check_vma=False)
```

time: 331 us -> 175 us (0.53)
  other arithmetic: 141 us -> 0 us
  Pallas kernels: 35.4 us -> 166 us
  waiting for transfers between devices: 64.5 us -> 0 us
  blocking collectives: 46.7 us -> 0 us
  starting transfers between devices: 24.6 us -> 0 us
  local copies, waits for them, and re-layouts: 12.1 us -> 8.23 us
    pallas_call x0 -> x3, Pallas kernels: none -> 140 us  [the longest x1 86.9 us: filtered_columns(): pl.pallas_call(functools.partial(filter_kernel, nb, nd), out_shape=(jax.S...]
    convert_element_type x4 -> x0, other arithmetic: 60.4 us -> none  [the longest x1 19.7 us: body(): second = (2.0 * sigma_two / width_e * centred(extend(first_iter), potenti...]
    another operation x9 -> x0, other arithmetic: 53.9 us -> none  [the longest x6 34 us: body(): lower_factor = jnp.linalg.cholesky(correlation)]
    all_to_all x1 -> x0, blocking collectives: 46.7 us -> none  [body(): lax.all_to_all(mixed, 'band', split_axis=0, concat_axis=1, tiled=True)]
    ppermute x6 -> x0, waiting for transfers between devices: 39.5 us -> none  [the longest x3 21.5 us: padded_2(): lax.ppermute(lax.slice_in_dim(block, 0, width, axis=dim), axis, backward)]
    concatenate x3 -> x0, other arithmetic: 26.2 us -> none  [padded_2(): block = jnp.concatenate([low, block, high], axis=dim)]
    all_to_all x1 -> x0, waiting for transfers between devices: 25 us -> none  [body(): lax.all_to_all(flattened, 'band', split_axis=1, concat_axis=0, tiled=True)]
    ppermute x6 -> x0, starting transfers between devices: 14.4 us -> none  [the longest x3 7.49 us: padded_2(): lax.ppermute(lax.slice_in_dim(block, 0, width, axis=dim), axis, backward)]
  transfers between devices with their start and end apart: 7 -> 0, of which waited for: 7 -> 0; matrix products, arithmetic and copies ran while one was open for 0% -> 0% of each run, Pallas kernels for 0% -> 0%
where the time goes in v2:
time: 175 us; the launch traced here: 174 us
  Pallas kernels  166 us (95%)
  local copies, waits for them, and re-layouts  8.23 us (5%)
    pallas_call x1, Pallas kernels, filtered_columns(): pl.pallas_call(functools.partial(filter_kernel, nb, nd), out_shape=(jax.S...  86.9 us
    pallas_call x1, Pallas kernels, rotated(): pl.pallas_call(functools.partial(rotate_kernel, nb), out_shape=jax.ShapeD...  42.5 us
    pallas_call x1, Pallas kernels, all_reduce(): pl.pallas_call(functools.partial(all_reduce_kernel, nx, ny, nzl, nzh), ou...  25.3 us
    pallas_call x1, Pallas kernels, rotation_of(): pl.pallas_call(functools.partial(rotation_kernel, panel, cells), out_shap...  10.8 us
    unnamed x13, local copies, waits for them, and re-layouts  6.48 us

profile of v2, /device:TPU:64, one launch (start us, length us, event | category | flops | bytes accessed | tf_op | source)
XLA Modules:
  0.0 173.8 jit_solution(10785578417715638326)
XLA Ops:
  0.0 0.8 copy.6.scale_ref
  0.8 0.0 copy-start
  0.8 1.4 copy-done
  2.2 0.0 copy-start.2
  2.2 1.0 copy-done.2
  3.1 0.0 copy-start.4
  3.1 0.9 copy-done.4
  4.0 0.0 copy-start.5
  4.0 0.8 copy-done.5
  4.9 86.9 %filter.1 = (bf16[24,256,128]{2,1,0:T(8,128)(2,1)S(1)}, f32[256,256]{1,0:T(8,128)S(1)}) custom-call(bf16[32,12,16,128]{3,2,1,0:T(8,128)(2,1)S(1)} %copy-done, f32[32,12]{1,0:T(8,128)S(1)} %copy.6.scale_ref, f32[12,16,128]{2,1,0:T(8,128)S(1)} %copy-done.4, bf16[384,384]{1,0:T(8,128)(2,1)S(1)} %copy-done.2, bf16[256,128]{1,0:T(8,128)(2,1)S(1)} %copy-done.5), custom_call_target="tpu_custom_call" | custom-call | tf_op jit(solution)/shard_map/filter/pallas_call | solution.py:419
  91.8 0.0 copy-start.3
  91.8 0.7 copy-done.3
  92.5 25.3 %correlation_sum.1.gram_ref = f32[256,256]{1,0:T(8,128)} custom-call(f32[256,256]{1,0:T(8,128)} %copy-done.3), custom_call_target="tpu_custom_call" | custom-call | tf_op jit(solution)/shard_map/correlation_sum/pallas_call | solution.py:135
  117.9 10.8 %rotation.1.rot_ref = bf16[256,256]{1,0:T(8,128)(2,1)} custom-call(f32[256,256]{1,0:T(8,128)} %correlation_sum.1.gram_ref), custom_call_target="tpu_custom_call" | custom-call | tf_op jit(solution)/shard_map/rotation/pallas_call | solution.py:201
  128.7 0.0 copy-start.1
  128.7 0.9 copy-done.1
  129.6 42.5 %rotate.1 = bf16[192,32,128]{2,1,0:T(8,128)(2,1)S(1)} custom-call(bf16[256,256]{1,0:T(8,128)(2,1)S(1)} %copy-done.1, bf16[24,256,128]{2,1,0:T(8,128)(2,1)S(1)} %get-tuple-element.8.cols_ref), custom_call_target="tpu_custom_call" | custom-call | tf_op jit(solution)/shard_map/rotate/pallas_call | solution.py:486
  172.0 1.8 %copy.7 = bf16[32,12,16,128]{3,2,1,0:T(8,128)(2,1)} copy(bf16[32,12,16,128]{3,0,2,1:T(8,128)(2,1)S(1)} %bitcast.3) | data formatting | bytes 3145728 | tf_op jit(solution)/shard_map/reshape | solution.py:506
Async XLA Ops:
  0.8 1.4 copy-start
  2.2 1.0 copy-start.2
  3.1 0.9 copy-start.4
  4.0 0.8 copy-start.5
  91.8 0.7 copy-start.3
  128.7 0.9 copy-start.1

commit v3 on v0

v3 whole, which is shorter than its diff:
```python
import functools

import jax
import jax.numpy as jnp
import ml_dtypes
import numpy as np
from jax import lax
from jax.experimental import pallas as pl
from jax.experimental.pallas import tpu as pltpu
from jax.sharding import PartitionSpec as P

MESH = pl.DeviceIdType.MESH

grid_step = 0.5
stencil_coef = (
    -5369.0 / 1800.0,
    12.0 / 7.0,
    -15.0 / 56.0,
    10.0 / 189.0,
    -1.0 / 112.0,
    2.0 / 1925.0,
    -1.0 / 16632.0,
)
lower_end = -4.0
cut_energy = 6.0
upper_end = 43.0


def filter_terms():
    width_e = (upper_end - cut_energy) / 2.0
    centre = (upper_end + cut_energy) / 2.0
    sigma_one = width_e / (lower_end - centre)
    gamma_term = 2.0 / sigma_one
    sigma_two = 1.0 / (gamma_term - sigma_one)
    sigma_three = 1.0 / (gamma_term - sigma_two)
    return (width_e, centre, sigma_one, sigma_two, sigma_three)


def remote(src, dst, send_sem, recv_sem, device):
    return pltpu.make_async_remote_copy(
        src_ref=src, dst_ref=dst, send_sem=send_sem, recv_sem=recv_sem,
        device_id=device, device_id_type=MESH,
    )


def stencil_matrices(planes, rows_y, rows_z):
    reach = len(stencil_coef) - 1
    kinetic = -0.5 / (grid_step * grid_step)
    plane_part = np.zeros((planes, rows_y, planes + 2 * reach, rows_y), np.float64)
    line_part = np.zeros((rows_z, rows_z), np.float64)
    for m in range(1, reach + 1):
        weight = kinetic * stencil_coef[m]
        for sign in (-m, m):
            for x in range(planes):
                for y in range(rows_y):
                    plane_part[x, y, x + reach + sign, y] += weight
                    if 0 <= y + sign < rows_y:
                        plane_part[x, y, x + reach, y + sign] += weight
            for z in range(rows_z):
                if 0 <= z + sign < rows_z:
                    line_part[z + sign, z] += weight
    plane_part = plane_part.reshape(planes * rows_y, (planes + 2 * reach) * rows_y)

    def halves(matrix):
        high = matrix.astype(ml_dtypes.bfloat16)
        low = (matrix - high.astype(np.float64)).astype(ml_dtypes.bfloat16)
        return np.concatenate([high, low], axis=0)

    return halves(plane_part), halves(line_part)


GROUP = 4
PACK = 8
LAG = 2
STEPS = 3
CHUNKS = 4
PANEL = 32


def step_kernel(
    nx, ny, nzl, nzh, cells,
    orb_hbm, scale_ref, pot_hbm, plane_hbm, line_hbm, out_ref,
    orb, pot, plane_mat, line_mat, ext0, ext1, ext2, full, turned, cols, energy,
    gram, half, rows, line, mine, work, rot, mixed,
    load_s, const_s, up_s, up_r, down_s, down_r, share_s, share_r,
    core_s, core_r, plane_s, plane_r, line_s, line_r, back_s, back_r, last_s, last_r, home_s, home_r,
):
    nb, nd = ny * nzh, nzl * nx * 2
    band = lax.axis_index("band")
    domain = lax.axis_index("domain")
    orbitals, planes, rows_y, rows_z = orb.shape
    reach = len(stencil_coef) - 1
    cells_xy = planes * rows_y
    part = cells_xy // nb
    groups = orbitals // GROUP
    packs = orbitals // PACK
    ext = (ext0, ext1, ext2)
    has_low, has_high = domain > 0, domain < nd - 1
    width_e, centre, sigma_one, sigma_two, sigma_three = filter_terms()
    kinetic = -0.5 / (grid_step * grid_step)

    y, z_hi = band // nzh, lax.rem(band, nzh)
    core = lax.rem(domain, 2)
    x = lax.rem(domain // 2, nx)
    z_lo = domain // (2 * nx)
    place = y * nx + x
    places = nx * ny
    level = z_hi * nzl + z_lo
    levels = nzl * nzh
    partner = (band, domain + 1 - 2 * core)

    def at_place(p):
        return ((p // nx) * nzh + z_hi, (z_lo * nx + lax.rem(p, nx)) * 2 + core)

    def at_level(l):
        return (y * nzh + l // nzl, (lax.rem(l, nzl) * nx + x) * 2 + core)

    def load(g):
        some = pl.ds(g * GROUP, GROUP)
        return pltpu.make_async_copy(orb_hbm.at[some], orb.at[some], load_s.at[g])

    constants = [
        pltpu.make_async_copy(source, target, const_s.at[i])
        for i, (source, target) in enumerate(((pot_hbm, pot), (plane_hbm, plane_mat), (line_hbm, line_mat)))
    ]
    load(0).start()
    for copy in constants:
        copy.start()
    for g in range(1, groups):
        load(g).start()

    barrier = pltpu.get_barrier_semaphore()

    def greet(device):
        pl.semaphore_signal(barrier, inc=1, device_id=device, device_id_type=MESH)

    @pl.when(has_low)
    def _():
        greet((band, domain - 1))

    @pl.when(has_high)
    def _():
        greet((band, domain + 1))

    for k in range(1, nb):
        greet((lax.rem(band + k, nb), domain))
    greet(partner)
    for k in range(1, places):
        greet(at_place(lax.rem(place + k, places)))
    for k in range(1, levels):
        greet(at_level(lax.rem(level + k, levels)))

    def scale_group(g):
        load(g).wait()

        def one(i, carry):
            o = g * GROUP + i
            for p in range(planes):
                ext0[o, reach + p] = (orb[o, p].astype(jnp.float32) * scale_ref[o, p]).astype(jnp.bfloat16)
            return carry

        lax.fori_loop(0, GROUP, one, 0)

    def upward(s, g):
        some = pl.ds(g * GROUP, GROUP)
        return remote(ext[s].at[some, pl.ds(planes, reach)], ext[s].at[some, pl.ds(0, reach)],
                      up_s.at[s, g], up_r.at[s, g], (band, domain + 1))

    def downward(s, g):
        some = pl.ds(g * GROUP, GROUP)
        return remote(ext[s].at[some, pl.ds(reach, reach)], ext[s].at[some, pl.ds(planes + reach, reach)],
                      down_s.at[s, g], down_r.at[s, g], (band, domain - 1))

    def send_edges(s, g):
        @pl.when(has_high)
        def _():
            upward(s, g).start()

        @pl.when(has_low)
        def _():
            downward(s, g).start()

    def await_edges(s, g):
        @pl.when(has_low)
        def _():
            upward(s, g).wait_recv()

        @pl.when(has_high)
        def _():
            downward(s, g).wait_recv()

    def apply(s, g):
        def pair(i, carry):
            o = g * GROUP + 2 * i
            sources = [ext[s][o + q].reshape((planes + 2 * reach) * rows_y, rows_z) for q in range(2)]
            both = jnp.concatenate(sources, axis=1)
            spread = jnp.dot(plane_mat[...], both, preferred_element_type=jnp.float32)
            spread = spread[:cells_xy] + spread[cells_xy:]
            first_row = reach * rows_y
            for q in range(2):
                middle = sources[q][first_row : first_row + cells_xy]
                along = jnp.dot(
                    jnp.concatenate([middle, middle], axis=1), line_mat[...], preferred_element_type=jnp.float32
                )
                total = spread[:, q * rows_z : (q + 1) * rows_z] + along + energy[...] * middle.astype(jnp.float32)
                if s == 0:
                    value = total * (sigma_one / width_e)
                else:
                    earlier = ext[s - 1][o + q, pl.ds(reach, planes)].reshape(cells_xy, rows_z).astype(jnp.float32)
                    if s == 1:
                        value = total * (2.0 * sigma_two / width_e) - (sigma_one * sigma_two) * earlier
                    else:
                        value = total * (2.0 * sigma_three / width_e) - (sigma_two * sigma_three) * earlier
                if s < 2:
                    ext[s + 1][o + q, pl.ds(reach, planes)] = value.astype(jnp.bfloat16).reshape(planes, rows_y, rows_z)
                else:
                    full[lax.rem(o, PACK) + q] = value
            return carry

        lax.fori_loop(0, GROUP // 2, pair, 0)

    def turn(h):
        def block(r, carry):
            at = pl.multiple_of(r * 8, 8)
            piece = full[:, pl.ds(at, 8), :]
            turned[h, pl.ds(at, 8)] = jnp.swapaxes(piece, 0, 1).astype(jnp.bfloat16)
            return carry

        lax.fori_loop(0, cells_xy // 8, block, 0)

    def share(h, k):
        target = lax.rem(band + k, nb)
        return remote(turned.at[h, pl.ds(target * part, part)], cols.at[band * packs + h],
                      share_s.at[h, k], share_r.at[h, k], (target, domain))

    scale_group(0)
    constants[0].wait()
    energy[...] = pot[...].reshape(cells_xy, rows_z) + (3.0 * stencil_coef[0] * kinetic - centre)
    pl.semaphore_wait(
        barrier, nb - 1 + places + levels - 1 + has_low.astype(jnp.int32) + has_high.astype(jnp.int32)
    )
    send_edges(0, 0)
    for g in range(1, LAG + 1):
        scale_group(g)
        send_edges(0, g)

    @pl.when(jnp.logical_not(has_low))
    def _():
        for s in range(STEPS):
            ext[s][:, :reach] = jnp.zeros((orbitals, reach, rows_y, rows_z), jnp.bfloat16)

    @pl.when(jnp.logical_not(has_high))
    def _():
        for s in range(STEPS):
            ext[s][:, planes + reach :] = jnp.zeros((orbitals, reach, rows_y, rows_z), jnp.bfloat16)

    for copy in constants[1:]:
        copy.wait()

    for t in range(groups + (STEPS - 1) * LAG):
        for s in range(STEPS):
            g = t - s * LAG
            if not 0 <= g < groups:
                continue
            await_edges(s, g)
            apply(s, g)
            if s < STEPS - 1:
                send_edges(s + 1, g)
            if s == 0 and g + LAG + 1 < groups:
                scale_group(g + LAG + 1)
                send_edges(0, g + LAG + 1)
            if s == STEPS - 1 and (g + 1) * GROUP % PACK == 0:
                h = g * GROUP // PACK
                turn(h)
                for k in range(1, nb):
                    share(h, k).start()
                cols[band * packs + h] = turned[h, pl.ds(band * part, part)]

    for h in range(packs):
        for k in range(1, nb):
            share(h, k).wait()

    total_orbitals = nb * orbitals

    def column(r):
        return cols[:, r].reshape(total_orbitals, rows_z)

    def gram_step(i, total):
        both = jnp.concatenate([column(2 * i), column(2 * i + 1)], axis=1)
        return total + lax.dot_general(both, both, (((1,), (1,)), ((), ())), preferred_element_type=jnp.float32)

    gram[...] = lax.fori_loop(0, part // 2, gram_step, jnp.zeros(gram.shape, jnp.float32))

    half_rows = total_orbitals // 2
    piece = half_rows // places
    mine_at = pl.multiple_of(core * half_rows, 8)
    other_at = pl.multiple_of((1 - core) * half_rows, 8)
    swap = remote(gram.at[pl.ds(other_at, half_rows)], half, core_s, core_r, partner)
    swap.start()
    swap.wait()
    half[...] += gram[pl.ds(mine_at, half_rows), :]

    copies = []
    for k in range(1, places):
        p = lax.rem(place + k, places)
        copy = remote(half.at[pl.ds(pl.multiple_of(p * piece, 8), piece)], rows.at[place],
                      plane_s.at[k], plane_r.at[k], at_place(p))
        copy.start()
        copies.append(copy)
    rows[place] = half[pl.ds(pl.multiple_of(place * piece, 8), piece), :]
    for copy in copies:
        copy.wait()
    total = rows[0]
    for k in range(1, places):
        total = total + rows[k]
    mine[...] = total

    copies = []
    for k in range(1, levels):
        l = lax.rem(level + k, levels)
        copy = remote(mine, line.at[level], line_s.at[k], line_r.at[k], at_level(l))
        copy.start()
        copies.append(copy)
    line[level] = mine[...]
    for copy in copies:
        copy.wait()
    total = line[0]
    for k in range(1, levels):
        total = total + line[k]
    own = pl.ds(pl.multiple_of(mine_at + place * piece, 8), piece)
    work[own, :] = total

    copies = []
    for k in range(1, places):
        p = lax.rem(place + k, places)
        copy = remote(work.at[own], work.at[own], back_s.at[k], back_r.at[k], at_place(p))
        copy.start()
        copies.append(copy)
    for copy in copies:
        copy.wait()
    span = pl.ds(mine_at, half_rows)
    final = remote(work.at[span], work.at[span], last_s, last_r, partner)
    final.start()
    final.wait()

    factor_inverse(cells, work, rot)

    rows_each = part // CHUNKS

    def home(c, k):
        target = lax.rem(band + k, nb)
        return remote(mixed.at[target, pl.ds(c * rows_each, rows_each)],
                      out_ref.at[pl.ds(band * part + c * rows_each, rows_each)],
                      home_s.at[c, k], home_r.at[c, k], (target, domain))

    for c in range(CHUNKS):
        def mix(i, carry):
            r = c * rows_each + 2 * i
            both = jnp.concatenate([column(r), column(r + 1)], axis=1)
            value = jnp.dot(rot[...], both, preferred_element_type=jnp.float32).astype(jnp.bfloat16)
            mixed[:, r] = value[:, :rows_z].reshape(nb, orbitals, rows_z)
            mixed[:, r + 1] = value[:, rows_z:].reshape(nb, orbitals, rows_z)
            return carry

        lax.fori_loop(0, rows_each // 2, mix, 0)
        for k in range(1, nb):
            home(c, k).start()

    out_ref[pl.ds(band * part, part)] = mixed[band]
    for c in range(CHUNKS):
        for k in range(1, nb):
            home(c, k).wait()
    for s in range(STEPS):
        for g in range(groups):
            @pl.when(has_high)
            def _():
                upward(s, g).wait_send()

            @pl.when(has_low)
            def _():
                downward(s, g).wait_send()


def factor_inverse(cells, work, out_ref):
    size = work.shape[0]
    panel = PANEL
    work[...] = work[...] * (1.0 / cells)
    lane = lax.broadcasted_iota(jnp.int32, (panel, size), 1)
    row = lax.broadcasted_iota(jnp.int32, (panel, size), 0)
    sub = lax.broadcasted_iota(jnp.int32, (panel, 128), 0)
    wide = lax.broadcasted_iota(jnp.int32, (size, size), 1)

    def step(k, carry):
        start = pl.multiple_of(k * panel, panel)
        tile = pl.multiple_of((start // 128) * 128, 128)
        here = pl.ds(start, panel)
        corner = pltpu.roll(work[here, pl.ds(tile, 128)], 128 - (start - tile), 1)
        rows = work[here, :]
        inside = (lane >= start) & (lane < start + panel)
        rows = jnp.where(inside, jnp.where(lane - start == row, 1.0, 0.0), rows)
        columns = [jnp.broadcast_to(corner[:, j : j + 1], (panel, 128)) for j in range(panel)]
        pivots = jnp.ones((panel, 128), jnp.float32)
        for j in range(panel):
            spread = [jnp.broadcast_to(columns[j][l : l + 1, :], (panel, 128)) for l in range(j, panel)]
            pivot = spread[0]
            pivots = jnp.where(sub == j, pivot, pivots)
            if j < panel - 1:
                factor = jnp.where(sub > j, columns[j] * (1.0 / pivot), 0.0)
                for l in range(j + 1, panel):
                    columns[l] = columns[l] - factor * spread[l - j]
                wide_factor = jnp.concatenate([factor] * (size // 128), axis=1)
                rows = rows - wide_factor * jnp.broadcast_to(rows[j : j + 1, :], (panel, size))
        scale = lax.rsqrt(pivots)
        rows = rows * jnp.concatenate([scale] * (size // 128), axis=1)
        below = jnp.where(lane >= start + panel, rows, 0.0)
        change = lax.dot_general(
            below, rows, (((0,), (0,)), ((), ())),
            precision=lax.Precision.HIGHEST, preferred_element_type=jnp.float32,
        )
        keep = (wide >= start) & (wide < start + panel)
        work[...] = jnp.where(keep, 0.0, work[...]) - change
        work[here, :] = rows
        return carry

    lax.fori_loop(0, size // panel, step, 0)
    down = lax.broadcasted_iota(jnp.int32, (size, size), 0)
    out_ref[...] = jnp.where(wide <= down, work[...], 0.0).astype(out_ref.dtype)


def fused_step(orbital_block, block_scale, potential, nx, ny, nzl, nzh):
    orbitals, planes, rows_y, rows_z = orbital_block.shape
    reach = len(stencil_coef) - 1
    plane_part, line_part = stencil_matrices(planes, rows_y, rows_z)
    cells_xy = planes * rows_y
    groups, packs = orbitals // GROUP, orbitals // PACK
    nb, nd = ny * nzh, nzl * nx * 2
    places, levels = nx * ny, nzl * nzh
    part, size = cells_xy // nb, nb * orbitals
    piece = size // 2 // places
    dma = pltpu.SemaphoreType.DMA
    f32, bf16 = jnp.float32, jnp.bfloat16
    hbm = pl.BlockSpec(memory_space=pl.ANY)
    wide = pltpu.VMEM((orbitals, planes + 2 * reach, rows_y, rows_z), bf16)
    edge = dma((STEPS, groups))
    return pl.pallas_call(
        functools.partial(step_kernel, nx, ny, nzl, nzh, float(cells_xy * rows_z * nd)),
        out_shape=jax.ShapeDtypeStruct((cells_xy, orbitals, rows_z), bf16),
        in_specs=[hbm, pl.BlockSpec(memory_space=pltpu.SMEM), hbm, hbm, hbm],
        out_specs=pl.BlockSpec(memory_space=pltpu.VMEM),
        scratch_shapes=[
            pltpu.VMEM(orbital_block.shape, bf16),
            pltpu.VMEM(potential.shape, f32),
            pltpu.VMEM(plane_part.shape, bf16),
            pltpu.VMEM(line_part.shape, bf16),
            wide, wide, wide,
            pltpu.VMEM((PACK, cells_xy, rows_z), f32),
            pltpu.VMEM((packs, cells_xy, PACK, rows_z), bf16),
            pltpu.VMEM((nb * packs, part, PACK, rows_z), bf16),
            pltpu.VMEM((cells_xy, rows_z), f32),
            pltpu.VMEM((size, size), f32),
            pltpu.VMEM((size // 2, size), f32),
            pltpu.VMEM((places, piece, size), f32),
            pltpu.VMEM((levels, piece, size), f32),
            pltpu.VMEM((piece, size), f32),
            pltpu.VMEM((size, size), f32),
            pltpu.VMEM((size, size), bf16),
            pltpu.VMEM((nb, part, orbitals, rows_z), bf16),
            dma((groups,)), dma((3,)), edge, edge, edge, edge, dma((packs, nb)), dma((packs, nb)),
            dma, dma, dma((places,)), dma((places,)), dma((levels,)), dma((levels,)),
            dma((places,)), dma((places,)), dma, dma, dma((CHUNKS, nb)), dma((CHUNKS, nb)),
        ],
        compiler_params=pltpu.CompilerParams(collective_id=1, has_side_effects=True, vmem_limit_bytes=60 << 20),
        name="filter_and_rotate",
    )(orbital_block, block_scale, potential, jnp.asarray(plane_part), jnp.asarray(line_part))


def solution(mesh):
    nzh, nzl, nx = 2, 4, 4
    ny = mesh.shape["band"] // nzh

    def body(orbital_block, block_scale, potential):
        back = fused_step(orbital_block, block_scale, potential, nx, ny, nzl, nzh)
        return back.transpose(1, 0, 2).reshape(orbital_block.shape)

    in_specs = (P("band", "domain", None, None), P("band", "domain"), P("domain", None, None))
    out_specs = P("band", "domain", None, None)
    return jax.shard_map(body, mesh=mesh, in_specs=in_specs, out_specs=out_specs, check_vma=False)
```

time: 567 us -> 151 us (0.27); the launches traced: 560 us -> 150 us
  waiting for transfers between devices: 298 us -> 0 us
  Pallas kernels: 0 us -> 146 us
  other arithmetic: 143 us -> 0 us
  blocking collectives: 77 us -> 0 us
  between operations: 15 us -> 0.01 us
  starting transfers between devices: 14.4 us -> 0 us
    psum x1 -> x0, waiting for transfers between devices: 258 us -> none  [body(): gram_sum = lax.psum(partial_gram, ('band', 'domain'))]
    pallas_call x0 -> x1, Pallas kernels: none -> 146 us  [fused_step(): pl.pallas_call(functools.partial(step_kernel, nx, ny, nzl, nzh, float(cel...]
    all_to_all x2 -> x0, blocking collectives: 77 us -> none  [the longest x1 42 us: body(): lax.all_to_all(mixed, 'band', split_axis=0, concat_axis=1, tiled=True)]
    convert_element_type x4 -> x0, other arithmetic: 60.4 us -> none  [the longest x1 19.7 us: body(): second = (2.0 * sigma_two / width_e * centred(extend(first_iter), potenti...]
    another operation x9 -> x0, other arithmetic: 54 us -> none  [the longest x6 34 us: body(): lower_factor = jnp.linalg.cholesky(correlation)]
    ppermute x6 -> x0, waiting for transfers between devices: 39.5 us -> none  [the longest x3 21.5 us: padded_2(): lax.ppermute(lax.slice_in_dim(block, 0, width, axis=dim), axis, backward)]
    concatenate x3 -> x0, other arithmetic: 26.2 us -> none  [padded_2(): block = jnp.concatenate([low, block, high], axis=dim)]
    ppermute x6 -> x0, starting transfers between devices: 14.4 us -> none  [the longest x3 7.49 us: padded_2(): lax.ppermute(lax.slice_in_dim(block, 0, width, axis=dim), axis, backward)]
  transfers between devices with their start and end apart: 7 -> 0, of which waited for: 7 -> 0; matrix products, arithmetic and copies ran while one was open for 0% -> 0% of each run, Pallas kernels for 0% -> 0%
where the time goes in v3:
time: 151 us; the launch traced here: 150 us
  Pallas kernels  146 us (97%)
  local copies, waits for them, and re-layouts  4.54 us (3%)
    pallas_call x1, Pallas kernels, fused_step(): pl.pallas_call(functools.partial(step_kernel, nx, ny, nzl, nzh, float(cel...  146 us
    reshape x1, local copies, waits for them, and re-layouts, body(): return back.transpose(1, 0, 2).reshape(orbital_block.shape)  3.16 us

profile of v3, /device:TPU:64, one launch (start us, length us, event | category | flops | bytes accessed | tf_op | source)
XLA Modules:
  0.0 150.5 jit_solution(2538833143484685675)
XLA Ops:
  0.0 1.4 copy.6.scale_ref
  1.4 145.9 %filter_and_rotate.1 = bf16[192,32,128]{2,1,0:T(8,128)(2,1)} custom-call(bf16[32,12,16,128]{3,2,1,0:T(8,128)(2,1)} %orb_hbm.1, f32[32,12]{1,0:T(8,128)} %copy.6.scale_ref, f32[12,16,128]{2,1,0:T(8,128)} %pot_hbm.1, bf16[384,384]{1,0:T(8,128)(2,1)} %constant.4.clone.plane_hbm, bf16[256,128]{1,0:T(8,128)(2,1)} %constant.5.clone.line_hbm), custom_call_target="tpu_custom_call" | custom-call | tf_op jit(solution)/shard_map/filter_and_rotate/pallas_call | solution.py:445
  147.3 3.2 %copy.7 = bf16[32,12,16,128]{3,2,1,0:T(8,128)(2,1)} copy(bf16[32,12,16,128]{3,0,2,1:T(8,128)(2,1)} %bitcast.3) | data formatting | bytes 3145728 | tf_op jit(solution)/shard_map/reshape | solution.py:483

commit v4 on v3

--- a/solution.py
+++ b/solution.py
@@ -45,11 +45,10 @@
 
 def stencil_matrices(planes, rows_y, rows_z):
     reach = len(stencil_coef) - 1
-    kinetic = -0.5 / (grid_step * grid_step)
     plane_part = np.zeros((planes, rows_y, planes + 2 * reach, rows_y), np.float64)
-    line_part = np.zeros((rows_z, rows_z), np.float64)
+    line_part = np.zeros((2, rows_z, 2, rows_z), np.float64)
     for m in range(1, reach + 1):
-        weight = kinetic * stencil_coef[m]
+        weight = stencil_coef[m] / stencil_coef[1]
         for sign in (-m, m):
             for x in range(planes):
                 for y in range(rows_y):
@@ -58,32 +57,31 @@
                         plane_part[x, y, x + reach, y + sign] += weight
             for z in range(rows_z):
                 if 0 <= z + sign < rows_z:
-                    line_part[z + sign, z] += weight
+                    for q in range(2):
+                        line_part[q, z + sign, q, z] += weight
     plane_part = plane_part.reshape(planes * rows_y, (planes + 2 * reach) * rows_y)
-
-    def halves(matrix):
-        high = matrix.astype(ml_dtypes.bfloat16)
-        low = (matrix - high.astype(np.float64)).astype(ml_dtypes.bfloat16)
-        return np.concatenate([high, low], axis=0)
-
-    return halves(plane_part), halves(line_part)
+    line_part = line_part.reshape(2 * rows_z, 2 * rows_z)
+    return plane_part.astype(ml_dtypes.bfloat16), line_part.astype(ml_dtypes.bfloat16)
 
 
 GROUP = 4
 PACK = 8
 LAG = 2
 STEPS = 3
-CHUNKS = 4
+CHUNKS = 8
+UNROLL = True
+AHEAD = 4
+EARLY = 8
 PANEL = 32
 
 
 def step_kernel(
     nx, ny, nzl, nzh, cells,
-    orb_hbm, scale_ref, pot_hbm, plane_hbm, line_hbm, out_ref,
-    orb, pot, plane_mat, line_mat, ext0, ext1, ext2, full, turned, cols, energy,
-    gram, half, rows, line, mine, work, rot, mixed,
+    orb_hbm, scale_hbm, pot_hbm, plane_hbm, line_hbm, out_ref,
+    orb, scale, spread_scale, pot, plane_mat, line_mat, ext0, ext1, ext2, full, turned, cols, energy,
+    gram, half, rows, line, mine, work, rot, rot_own, mixed,
     load_s, const_s, up_s, up_r, down_s, down_r, share_s, share_r,
-    core_s, core_r, plane_s, plane_r, line_s, line_r, back_s, back_r, last_s, last_r, home_s, home_r,
+    core_s, core_r, plane_s, plane_r, line_s, line_r, back_s, back_r, last_s, last_r, home_s, home_r, ahead_s, ahead_r,
 ):
     nb, nd = ny * nzh, nzl * nx * 2
     band = lax.axis_index("band")
@@ -121,10 +119,11 @@
 
     constants = [
         pltpu.make_async_copy(source, target, const_s.at[i])
-        for i, (source, target) in enumerate(((pot_hbm, pot), (plane_hbm, plane_mat), (line_hbm, line_mat)))
+        for i, (source, target) in enumerate(((scale_hbm, scale), (pot_hbm, pot), (plane_hbm, plane_mat), (line_hbm, line_mat)))
     ]
+    constants[0].start()
     load(0).start()
-    for copy in constants:
+    for copy in constants[1:]:
         copy.start()
     for g in range(1, groups):
         load(g).start()
@@ -156,7 +155,7 @@
         def one(i, carry):
             o = g * GROUP + i
             for p in range(planes):
-                ext0[o, reach + p] = (orb[o, p].astype(jnp.float32) * scale_ref[o, p]).astype(jnp.bfloat16)
+                ext0[o, reach + p] = (orb[o, p].astype(jnp.float32) * spread_scale[p, pl.ds(o, 1), :]).astype(jnp.bfloat16)
             return carry
 
         lax.fori_loop(0, GROUP, one, 0)
@@ -188,36 +187,32 @@
         @pl.when(has_high)
         def _():
             downward(s, g).wait_recv()
+
+    outer = (sigma_one / width_e, 2.0 * sigma_two / width_e, 2.0 * sigma_three / width_e)
+    inner = (None, sigma_one * sigma_two, sigma_two * sigma_three)
 
     def apply(s, g):
         def pair(i, carry):
             o = g * GROUP + 2 * i
             sources = [ext[s][o + q].reshape((planes + 2 * reach) * rows_y, rows_z) for q in range(2)]
             both = jnp.concatenate(sources, axis=1)
+            middle = both[reach * rows_y : reach * rows_y + cells_xy]
             spread = jnp.dot(plane_mat[...], both, preferred_element_type=jnp.float32)
-            spread = spread[:cells_xy] + spread[cells_xy:]
-            first_row = reach * rows_y
+            spread = spread + jnp.dot(middle, line_mat[...], preferred_element_type=jnp.float32)
             for q in range(2):
-                middle = sources[q][first_row : first_row + cells_xy]
-                along = jnp.dot(
-                    jnp.concatenate([middle, middle], axis=1), line_mat[...], preferred_element_type=jnp.float32
-                )
-                total = spread[:, q * rows_z : (q + 1) * rows_z] + along + energy[...] * middle.astype(jnp.float32)
-                if s == 0:
-                    value = total * (sigma_one / width_e)
-                else:
-                    earlier = ext[s - 1][o + q, pl.ds(reach, planes)].reshape(cells_xy, rows_z).astype(jnp.float32)
-                    if s == 1:
-                        value = total * (2.0 * sigma_two / width_e) - (sigma_one * sigma_two) * earlier
-                    else:
-                        value = total * (2.0 * sigma_three / width_e) - (sigma_two * sigma_three) * earlier
-                if s < 2:
+                lanes = slice(q * rows_z, (q + 1) * rows_z)
+                value = spread[:, lanes] * (outer[s] * kinetic * stencil_coef[1])
+                value = value + energy[s] * middle[:, lanes].astype(jnp.float32)
+                if s > 0:
+                    earlier = ext[s - 1][o + q, pl.ds(reach, planes)].reshape(cells_xy, rows_z)
+                    value = value - inner[s] * earlier.astype(jnp.float32)
+                if s < STEPS - 1:
                     ext[s + 1][o + q, pl.ds(reach, planes)] = value.astype(jnp.bfloat16).reshape(planes, rows_y, rows_z)
                 else:
                     full[lax.rem(o, PACK) + q] = value
             return carry
 
-        lax.fori_loop(0, GROUP // 2, pair, 0)
+        lax.fori_loop(0, GROUP // 2, pair, 0, unroll=UNROLL)
 
     def turn(h):
         def block(r, carry):
@@ -228,20 +223,44 @@
 
         lax.fori_loop(0, cells_xy // 8, block, 0)
 
-    def share(h, k):
-        target = lax.rem(band + k, nb)
-        return remote(turned.at[h, pl.ds(target * part, part)], cols.at[band * packs + h],
-                      share_s.at[h, k], share_r.at[h, k], (target, domain))
-
-    scale_group(0)
+    span_rows = part * nzh
+    my_rows = pl.ds(pl.multiple_of(z_hi * part, 8), part)
+
+    def same_share(h, k):
+        target = lax.rem(y + k, ny)
+        return remote(turned.at[h, pl.ds(target * span_rows, span_rows)], cols.at[band * packs + h],
+                      share_s.at[h, k], share_r.at[h, k], (target * nzh + z_hi, domain))
+
+    def cross_share(h, k):
+        target = lax.rem(y + k, ny)
+        there = 1 - z_hi
+        rows_there = pl.ds(pl.multiple_of(there * part, 8), part)
+        return remote(turned.at[h, pl.ds(pl.multiple_of((target * nzh + there) * part, 8), part)],
+                      cols.at[band * packs + h, rows_there],
+                      share_s.at[h, ny + k], share_r.at[h, ny + k], (target * nzh + there, domain))
+
+    def shares(h):
+        return [cross_share(h, k) for k in range(ny)] + [same_share(h, k) for k in range(1, ny)]
+
+    def ahead(i):
+        pack = (2 * (i // packs) + z_hi) * packs + i % packs
+        return remote(cols.at[pack, my_rows], cols.at[pack, my_rows], ahead_s.at[i], ahead_r.at[i],
+                      (y * nzh + 1 - z_hi, domain))
+
     constants[0].wait()
-    energy[...] = pot[...].reshape(cells_xy, rows_z) + (3.0 * stencil_coef[0] * kinetic - centre)
+    upright = scale[...].T
+    for p in range(planes):
+        spread_scale[p] = jnp.broadcast_to(upright[:, p : p + 1], (orbitals, rows_z))
+    for g in range(EARLY):
+        scale_group(g)
+    constants[1].wait()
+    shifted = pot[...].reshape(cells_xy, rows_z) + (3.0 * stencil_coef[0] * kinetic - centre)
+    for s in range(STEPS):
+        energy[s] = shifted * outer[s]
     pl.semaphore_wait(
         barrier, nb - 1 + places + levels - 1 + has_low.astype(jnp.int32) + has_high.astype(jnp.int32)
     )
-    send_edges(0, 0)
-    for g in range(1, LAG + 1):
-        scale_group(g)
+    for g in range(LAG + 1):
         send_edges(0, g)
 
     @pl.when(jnp.logical_not(has_low))
@@ -254,7 +273,7 @@
         for s in range(STEPS):
             ext[s][:, planes + reach :] = jnp.zeros((orbitals, reach, rows_y, rows_z), jnp.bfloat16)
 
-    for copy in constants[1:]:
+    for copy in constants[2:]:
         copy.wait()
 
     for t in range(groups + (STEPS - 1) * LAG):
@@ -267,18 +286,21 @@
             if s < STEPS - 1:
                 send_edges(s + 1, g)
             if s == 0 and g + LAG + 1 < groups:
-                scale_group(g + LAG + 1)
+                if g + LAG + 1 >= EARLY:
+                    scale_group(g + LAG + 1)
                 send_edges(0, g + LAG + 1)
             if s == STEPS - 1 and (g + 1) * GROUP % PACK == 0:
                 h = g * GROUP // PACK
                 turn(h)
-                for k in range(1, nb):
-                    share(h, k).start()
-                cols[band * packs + h] = turned[h, pl.ds(band * part, part)]
+                for copy in shares(h):
+                    copy.start()
+                cols[band * packs + h] = turned[h, pl.ds(y * span_rows, span_rows)]
 
     for h in range(packs):
-        for k in range(1, nb):
-            share(h, k).wait()
+        for copy in shares(h):
+            copy.wait()
+    for i in range(AHEAD):
+        ahead(i).start()
 
     total_orbitals = nb * orbitals
 
@@ -286,7 +308,8 @@
         return cols[:, r].reshape(total_orbitals, rows_z)
 
     def gram_step(i, total):
-        both = jnp.concatenate([column(2 * i), column(2 * i + 1)], axis=1)
+        r = z_hi * part + 2 * i
+        both = jnp.concatenate([column(r), column(r + 1)], axis=1)
         return total + lax.dot_general(both, both, (((1,), (1,)), ((), ())), preferred_element_type=jnp.float32)
 
     gram[...] = lax.fori_loop(0, part // 2, gram_step, jnp.zeros(gram.shape, jnp.float32))
@@ -324,6 +347,8 @@
     line[level] = mine[...]
     for copy in copies:
         copy.wait()
+    for i in range(AHEAD, ny * packs):
+        ahead(i).start()
     total = line[0]
     for k in range(1, levels):
         total = total + line[k]
@@ -345,30 +370,40 @@
 
     factor_inverse(cells, work, rot)
 
-    rows_each = part // CHUNKS
+    for k in range(ny):
+        rot_own[pl.ds(k * orbitals, orbitals), :] = rot[pl.ds(pl.multiple_of((k * nzh + z_hi) * orbitals, orbitals), orbitals), :]
+    rows_each = span_rows // CHUNKS
+
+    def chunk_row(c):
+        return pl.multiple_of(lax.rem(z_hi * part + c * rows_each, span_rows), 2)
 
     def home(c, k):
-        target = lax.rem(band + k, nb)
-        return remote(mixed.at[target, pl.ds(c * rows_each, rows_each)],
-                      out_ref.at[pl.ds(band * part + c * rows_each, rows_each)],
-                      home_s.at[c, k], home_r.at[c, k], (target, domain))
+        target = lax.rem(y + k, ny)
+        first = chunk_row(c)
+        return remote(mixed.at[target, pl.ds(first, rows_each)],
+                      out_ref.at[pl.ds(y * span_rows + first, rows_each)],
+                      home_s.at[c, k], home_r.at[c, k], (target * nzh + z_hi, domain))
 
     for c in range(CHUNKS):
+        if c == CHUNKS // 2:
+            for i in range(ny * packs):
+                ahead(i).wait()
+
         def mix(i, carry):
-            r = c * rows_each + 2 * i
+            r = chunk_row(c) + 2 * i
             both = jnp.concatenate([column(r), column(r + 1)], axis=1)
-            value = jnp.dot(rot[...], both, preferred_element_type=jnp.float32).astype(jnp.bfloat16)
-            mixed[:, r] = value[:, :rows_z].reshape(nb, orbitals, rows_z)
-            mixed[:, r + 1] = value[:, rows_z:].reshape(nb, orbitals, rows_z)
+            value = jnp.dot(rot_own[...], both, preferred_element_type=jnp.float32).astype(jnp.bfloat16)
+            mixed[:, r] = value[:, :rows_z].reshape(ny, orbitals, rows_z)
+            mixed[:, r + 1] = value[:, rows_z:].reshape(ny, orbitals, rows_z)
             return carry
 
         lax.fori_loop(0, rows_each // 2, mix, 0)
-        for k in range(1, nb):
+        for k in range(1, ny):
             home(c, k).start()
 
-    out_ref[pl.ds(band * part, part)] = mixed[band]
+    out_ref[pl.ds(y * span_rows, span_rows)] = mixed[y]
     for c in range(CHUNKS):
-        for k in range(1, nb):
+        for k in range(1, ny):
             home(c, k).wait()
     for s in range(STEPS):
         for g in range(groups):
@@ -439,24 +474,26 @@
     piece = size // 2 // places
     dma = pltpu.SemaphoreType.DMA
     f32, bf16 = jnp.float32, jnp.bfloat16
-    hbm = pl.BlockSpec(memory_space=pl.ANY)
+    hbm = pl.BlockSpec(memory_space=pltpu.HBM)
     wide = pltpu.VMEM((orbitals, planes + 2 * reach, rows_y, rows_z), bf16)
     edge = dma((STEPS, groups))
     return pl.pallas_call(
         functools.partial(step_kernel, nx, ny, nzl, nzh, float(cells_xy * rows_z * nd)),
         out_shape=jax.ShapeDtypeStruct((cells_xy, orbitals, rows_z), bf16),
-        in_specs=[hbm, pl.BlockSpec(memory_space=pltpu.SMEM), hbm, hbm, hbm],
+        in_specs=[hbm] * 5,
         out_specs=pl.BlockSpec(memory_space=pltpu.VMEM),
         scratch_shapes=[
             pltpu.VMEM(orbital_block.shape, bf16),
+            pltpu.VMEM(block_scale.shape[::-1], f32),
+            pltpu.VMEM((planes, orbitals, rows_z), f32),
             pltpu.VMEM(potential.shape, f32),
             pltpu.VMEM(plane_part.shape, bf16),
             pltpu.VMEM(line_part.shape, bf16),
             wide, wide, wide,
             pltpu.VMEM((PACK, cells_xy, rows_z), f32),
             pltpu.VMEM((packs, cells_xy, PACK, rows_z), bf16),
-            pltpu.VMEM((nb * packs, part, PACK, rows_z), bf16),
-            pltpu.VMEM((cells_xy, rows_z), f32),
+            pltpu.VMEM((nb * packs, part * nzh, PACK, rows_z), bf16),
+            pltpu.VMEM((STEPS, cells_xy, rows_z), f32),
             pltpu.VMEM((size, size), f32),
             pltpu.VMEM((size // 2, size), f32),
             pltpu.VMEM((places, piece, size), f32),
@@ -464,14 +501,16 @@
             pltpu.VMEM((piece, size), f32),
             pltpu.VMEM((size, size), f32),
             pltpu.VMEM((size, size), bf16),
-            pltpu.VMEM((nb, part, orbitals, rows_z), bf16),
-            dma((groups,)), dma((3,)), edge, edge, edge, edge, dma((packs, nb)), dma((packs, nb)),
+            pltpu.VMEM((ny * orbitals, size), bf16),
+            pltpu.VMEM((ny, part * nzh, orbitals, rows_z), bf16),
+            dma((groups,)), dma((4,)), edge, edge, edge, edge, dma((packs, nb)), dma((packs, nb)),
             dma, dma, dma((places,)), dma((places,)), dma((levels,)), dma((levels,)),
-            dma((places,)), dma((places,)), dma, dma, dma((CHUNKS, nb)), dma((CHUNKS, nb)),
+            dma((places,)), dma((places,)), dma, dma, dma((CHUNKS, ny)), dma((CHUNKS, ny)),
+            dma((ny * packs,)), dma((ny * packs,)),
         ],
-        compiler_params=pltpu.CompilerParams(collective_id=1, has_side_effects=True, vmem_limit_bytes=60 << 20),
+        compiler_params=pltpu.CompilerParams(collective_id=1, has_side_effects=True, vmem_limit_bytes=56 << 20),
         name="filter_and_rotate",
-    )(orbital_block, block_scale, potential, jnp.asarray(plane_part), jnp.asarray(line_part))
+    )(orbital_block, block_scale.T, potential, jnp.asarray(plane_part), jnp.asarray(line_part))
 
 
 def solution(mesh):

time: 151 us -> 137 us (0.907)
  Pallas kernels: 146 us -> 134 us
    pallas_call x1, Pallas kernels: 146 us -> 134 us  [fused_step(): pl.pallas_call(functools.partial(step_kernel, nx, ny, nzl, nzh, float(cel...]
where the time goes in v4:
time: 137 us
  Pallas kernels  134 us (98%)
  local copies, waits for them, and re-layouts  3.16 us (2%)
    pallas_call x1, Pallas kernels, fused_step(): pl.pallas_call(functools.partial(step_kernel, nx, ny, nzl, nzh, float(cel...  134 us
    reshape x1, local copies, waits for them, and re-layouts, body(): return back.transpose(1, 0, 2).reshape(orbital_block.shape)  3.16 us

profile of v4, /device:TPU:64, one launch (start us, length us, event | category | flops | bytes accessed | tf_op | source)
XLA Modules:
  0.0 137.0 jit_solution(700264052314548737)
XLA Ops:
  0.0 133.8 %filter_and_rotate.1 = bf16[192,32,128]{2,1,0:T(8,128)(2,1)} custom-call(bf16[32,12,16,128]{3,2,1,0:T(8,128)(2,1)} %orb_hbm.1, f32[12,32]{1,0:T(8,128)} %bitcast.5, f32[12,16,128]{2,1,0:T(8,128)} %pot_hbm.1, bf16[192,384]{1,0:T(8,128)(2,1)} %constant.4.clone.plane_hbm, bf16[256,256]{1,0:T(8,128)(2,1)} %constant.5.clone.line_hbm), custom_call_target="tpu_custom_call" | custom-call | tf_op jit(solution)/shard_map/filter_and_rotate/pallas_call | solution.py:480
  133.9 3.2 %copy.6 = bf16[32,12,16,128]{3,2,1,0:T(8,128)(2,1)} copy(bf16[32,12,16,128]{3,0,2,1:T(8,128)(2,1)} %bitcast.4) | data formatting | bytes 3145728 | tf_op jit(solution)/shard_map/reshape | solution.py:522

commit v5 on v4

--- a/solution.py
+++ b/solution.py
@@ -66,11 +66,11 @@
 
 GROUP = 4
 PACK = 8
-LAG = 2
+LAG = 3
 STEPS = 3
-CHUNKS = 8
+CHUNKS = 12
 UNROLL = True
-AHEAD = 4
+AHEAD = 1
 EARLY = 8
 PANEL = 32
 
@@ -242,10 +242,34 @@
     def shares(h):
         return [cross_share(h, k) for k in range(ny)] + [same_share(h, k) for k in range(1, ny)]
 
-    def ahead(i):
-        pack = (2 * (i // packs) + z_hi) * packs + i % packs
-        return remote(cols.at[pack, my_rows], cols.at[pack, my_rows], ahead_s.at[i], ahead_r.at[i],
-                      (y * nzh + 1 - z_hi, domain))
+    rows_each = span_rows // CHUNKS
+    blocks = part // rows_each
+    opposite = (y * nzh + 1 - z_hi, domain)
+
+    def ahead(i, k):
+        rows_i = pl.ds(pl.multiple_of(z_hi * part + i * rows_each, 2), rows_each)
+        block = cols.at[pl.ds((k * nzh + z_hi) * packs, packs), rows_i]
+        return remote(block, block, ahead_s.at[i, k], ahead_r.at[i, k], opposite)
+
+    def ahead_start(i):
+        for k in range(ny - 1):
+            ahead(i, k).start()
+
+        @pl.when(z_hi == 0)
+        def _():
+            ahead(i, ny - 1).start()
+
+    def ahead_wait(i):
+        for k in range(ny - 1):
+            ahead(i, k).wait()
+
+        @pl.when(z_hi == 0)
+        def _():
+            ahead(i, ny - 1).wait_send()
+
+        @pl.when(z_hi == 1)
+        def _():
+            ahead(i, ny - 1).wait_recv()
 
     constants[0].wait()
     upright = scale[...].T
@@ -300,7 +324,12 @@
         for copy in shares(h):
             copy.wait()
     for i in range(AHEAD):
-        ahead(i).start()
+        ahead_start(i)
+
+    @pl.when(z_hi == 0)
+    def _():
+        cols[pl.ds((nb - 1) * packs, packs), pl.ds(part, part)] = jnp.zeros((packs, part, PACK, rows_z), jnp.bfloat16)
+
 
     total_orbitals = nb * orbitals
 
@@ -347,8 +376,8 @@
     line[level] = mine[...]
     for copy in copies:
         copy.wait()
-    for i in range(AHEAD, ny * packs):
-        ahead(i).start()
+    for i in range(AHEAD, blocks):
+        ahead_start(i)
     total = line[0]
     for k in range(1, levels):
         total = total + line[k]
@@ -372,8 +401,6 @@
 
     for k in range(ny):
         rot_own[pl.ds(k * orbitals, orbitals), :] = rot[pl.ds(pl.multiple_of((k * nzh + z_hi) * orbitals, orbitals), orbitals), :]
-    rows_each = span_rows // CHUNKS
-
     def chunk_row(c):
         return pl.multiple_of(lax.rem(z_hi * part + c * rows_each, span_rows), 2)
 
@@ -385,9 +412,8 @@
                       home_s.at[c, k], home_r.at[c, k], (target * nzh + z_hi, domain))
 
     for c in range(CHUNKS):
-        if c == CHUNKS // 2:
-            for i in range(ny * packs):
-                ahead(i).wait()
+        if c >= blocks:
+            ahead_wait(c - blocks)
 
         def mix(i, carry):
             r = chunk_row(c) + 2 * i
@@ -506,7 +532,7 @@
             dma((groups,)), dma((4,)), edge, edge, edge, edge, dma((packs, nb)), dma((packs, nb)),
             dma, dma, dma((places,)), dma((places,)), dma((levels,)), dma((levels,)),
             dma((places,)), dma((places,)), dma, dma, dma((CHUNKS, ny)), dma((CHUNKS, ny)),
-            dma((ny * packs,)), dma((ny * packs,)),
+            dma((CHUNKS // nzh, ny)), dma((CHUNKS // nzh, ny)),
         ],
         compiler_params=pltpu.CompilerParams(collective_id=1, has_side_effects=True, vmem_limit_bytes=56 << 20),
         name="filter_and_rotate",

time: 137 us -> 136 us (level); the launches traced: 137 us -> 133 us
  Pallas kernels: 134 us -> 130 us
    pallas_call x1, Pallas kernels: 134 us -> 130 us  [fused_step(): pl.pallas_call(functools.partial(step_kernel, nx, ny, nzl, nzh, float(cel...]
where the time goes in v5:
time: 136 us; the launch traced here: 133 us
  Pallas kernels  130 us (96%)
  local copies, waits for them, and re-layouts  3.16 us (2%)
    pallas_call x1, Pallas kernels, fused_step(): pl.pallas_call(functools.partial(step_kernel, nx, ny, nzl, nzh, float(cel...  130 us
    reshape x1, local copies, waits for them, and re-layouts, body(): return back.transpose(1, 0, 2).reshape(orbital_block.shape)  3.16 us

profile of v5, /device:TPU:64, one launch (start us, length us, event | category | flops | bytes accessed | tf_op | source)
XLA Modules:
  0.0 133.1 jit_solution(1592785506521865880)
XLA Ops:
  0.0 129.9 %filter_and_rotate.1 = bf16[192,32,128]{2,1,0:T(8,128)(2,1)} custom-call(bf16[32,12,16,128]{3,2,1,0:T(8,128)(2,1)} %orb_hbm.1, f32[12,32]{1,0:T(8,128)} %bitcast.5, f32[12,16,128]{2,1,0:T(8,128)} %pot_hbm.1, bf16[192,384]{1,0:T(8,128)(2,1)} %constant.4.clone.plane_hbm, bf16[256,256]{1,0:T(8,128)(2,1)} %constant.5.clone.line_hbm), custom_call_target="tpu_custom_call" | custom-call | tf_op jit(solution)/shard_map/filter_and_rotate/pallas_call | solution.py:506
  129.9 3.2 %copy.6 = bf16[32,12,16,128]{3,2,1,0:T(8,128)(2,1)} copy(bf16[32,12,16,128]{3,0,2,1:T(8,128)(2,1)} %bitcast.4) | data formatting | bytes 3145728 | tf_op jit(solution)/shard_map/reshape | solution.py:548

commit v6 on v5

--- a/solution.py
+++ b/solution.py
@@ -70,7 +70,7 @@
 STEPS = 3
 CHUNKS = 12
 UNROLL = True
-AHEAD = 1
+AHEAD = 0
 EARLY = 8
 PANEL = 32
 

time: 136 us -> 133 us (0.978)
  Pallas kernels: 130 us -> 128 us
    pallas_call x1, Pallas kernels: 130 us -> 128 us  [fused_step(): pl.pallas_call(functools.partial(step_kernel, nx, ny, nzl, nzh, float(cel...]
where the time goes in v6:
time: 133 us; the launch traced here: 131 us
  Pallas kernels  128 us (96%)
  local copies, waits for them, and re-layouts  3.16 us (2%)
    pallas_call x1, Pallas kernels, fused_step(): pl.pallas_call(functools.partial(step_kernel, nx, ny, nzl, nzh, float(cel...  128 us
    reshape x1, local copies, waits for them, and re-layouts, body(): return back.transpose(1, 0, 2).reshape(orbital_block.shape)  3.16 us

profile of v6, /device:TPU:64, one launch (start us, length us, event | category | flops | bytes accessed | tf_op | source)
XLA Modules:
  0.0 131.4 jit_solution(11493769391346288556)
XLA Ops:
  0.0 128.3 %filter_and_rotate.1 = bf16[192,32,128]{2,1,0:T(8,128)(2,1)} custom-call(bf16[32,12,16,128]{3,2,1,0:T(8,128)(2,1)} %orb_hbm.1, f32[12,32]{1,0:T(8,128)} %bitcast.5, f32[12,16,128]{2,1,0:T(8,128)} %pot_hbm.1, bf16[192,384]{1,0:T(8,128)(2,1)} %constant.4.clone.plane_hbm, bf16[256,256]{1,0:T(8,128)(2,1)} %constant.5.clone.line_hbm), custom_call_target="tpu_custom_call" | custom-call | tf_op jit(solution)/shard_map/filter_and_rotate/pallas_call | solution.py:506
  128.3 3.2 %copy.6 = bf16[32,12,16,128]{3,2,1,0:T(8,128)(2,1)} copy(bf16[32,12,16,128]{3,0,2,1:T(8,128)(2,1)} %bitcast.4) | data formatting | bytes 3145728 | tf_op jit(solution)/shard_map/reshape | solution.py:548
